TPU v7x, 256 devices: a whole 4x4x8 slice. The times are simulated.
256 devices in a mesh: seq: 64 (over z, x, y_hi), head: 4 (over y_lo, core).
Axes of the slice: x: 4, y: 4 (y_hi: 2, y_lo: 2; y = y_hi * 2 + y_lo), z: 8, core: 2. Of those that a mesh axis runs over, the one named last changes fastest.
Arguments:
- hidden_in: bfloat16 [8192, 2048], P('seq'), may hold values from -6 to 6
- attn_gain: float32 [2048], replicated, may hold values from 0.1 to 1.9
- w_query: bfloat16 [2048, 3072], P(None, 'head'), may hold values from -2 to 2
- w_latent: bfloat16 [2048, 576], P(None, 'head'), may hold values from -2 to 2
- latent_gain: float32 [512], replicated, may hold values from 0.1 to 1.9
- w_expand: bfloat16 [512, 4096], P(None, 'head'), may hold values from -0.25 to 0.25
- w_out: bfloat16 [2048, 2048], P('head'), may hold values from -0.125 to 0.125
- moe_gain: float32 [2048], replicated, may hold values from 0.1 to 1.9
- w_gate: bfloat16 [64, 2048, 1408], P('seq', None, 'head'), may hold values from -0.125 to 0.125
- w_up: bfloat16 [64, 2048, 1408], P('seq', None, 'head'), may hold values from -0.125 to 0.125
- w_down: bfloat16 [64, 1408, 2048], P('seq', 'head'), may hold values from -0.15625 to 0.15625
- routes: int32 [8192, 6], P('seq'), may hold values from 0 to 63, all different within a row; in each aligned block of 128 rows (0 to 127, 128 to 255, ...) at most 15 rows name the same one
- gates: float32 [8192, 6], P('seq'), may hold values from 0.1 to 0.6
- segment: int32 [8192], P('seq'), may hold values from 0 to 16, never falling along the last dimension, each value on 1 to 6144 neighbouring positions
- page_table: int32 [64, 4], P('seq'), may hold values from 0 to 3, each once within a row
Outputs:
- hidden_out: bfloat16 [8192, 2048], P('seq')
- latent_cache: bfloat16 [256, 18432], P(('seq', 'head'))
Inputs may be any that keep to these rules, and one draw needn't show every extreme that they name: `routes`: each row names 6 different experts; among the 128 rows of one device no expert is named more than 15 times, a bound that some block reaches. `segment`: ids never fall along the stream; each of the 17 documents is contiguous, and the longest has exactly 6144 tokens. `page_table`: each row is a permutation of the 4 slots of one token block.
All inputs are finite; a program needn't handle non-finite values.
Results may differ from a plain program's by a relative error of at most 0.015.
Values may be sent and summed in bfloat16 or wider, within the bound.
A program may use at most 192 MiB of HBM per device.

v0:
```python
import jax
import jax.numpy as jnp
from jax import lax
from jax.sharding import PartitionSpec as P

D = 2048
NOPE = 128
ROPE = 64
VDIM = 128
LATENT = 512
TOPK = 6
PAGE = 32


EPS = 1e-06
THETA = 50000.0


def rms_scale(values, scale_gain):
    mean_sq = jnp.mean(values * values, axis=-1, keepdims=True)
    return values * lax.rsqrt(mean_sq + EPS) * scale_gain


def rope_tables(positions, feat_width):
    half_width = feat_width // 2
    inv_freq = THETA ** (-jnp.arange(half_width, dtype=jnp.float32) * 2.0 / feat_width)
    angles = positions.astype(jnp.float32)[:, None] * inv_freq[None, :]
    return (jnp.cos(angles), jnp.sin(angles))


def rotate(values, cosine, sine_table):
    half_width = values.shape[-1] // 2
    table_shape = cosine.shape[:1] + (1,) * (values.ndim - 2) + cosine.shape[1:]
    cosine = cosine.reshape(table_shape)
    sine_table = sine_table.reshape(table_shape)
    lower_half = values[..., :half_width]
    upper_half = values[..., half_width:]
    return jnp.concatenate(
        [
            lower_half * cosine - upper_half * sine_table,
            upper_half * cosine + lower_half * sine_table,
        ],
        axis=-1,
    )


def local(
    hidden_in,
    attn_gain,
    w_query,
    w_latent,
    latent_gain,
    w_expand,
    w_out,
    moe_gain,
    w_gate,
    w_up,
    w_down,
    routes,
    gates,
    segment,
    page_table,
):
    tok_rows = hidden_in.shape[0]
    local_heads = w_out.shape[0] // VDIM
    seq_index = lax.axis_index("seq")
    head_index = lax.axis_index("head")
    first_row = seq_index * tok_rows
    positions = first_row + jnp.arange(tok_rows, dtype=jnp.int32)
    cosine, sine_table = rope_tables(positions, ROPE)
    residual_in = hidden_in.astype(jnp.float32)
    normed = rms_scale(residual_in, attn_gain).astype(jnp.bfloat16)
    latent_part = jnp.dot(normed, w_latent, preferred_element_type=jnp.float32).astype(jnp.bfloat16)
    latent_raw = lax.all_gather(latent_part, "head", axis=1, tiled=True)
    compressed = rms_scale(latent_raw[:, :LATENT].astype(jnp.float32), latent_gain).astype(
        jnp.bfloat16
    )
    key_rope = rotate(latent_raw[:, LATENT:].astype(jnp.float32), cosine, sine_table).astype(
        jnp.bfloat16
    )
    queries = jnp.dot(normed, w_query, preferred_element_type=jnp.float32).reshape(
        tok_rows, local_heads, NOPE + ROPE
    )
    query_nope = queries[:, :, :NOPE].astype(jnp.bfloat16)
    query_rope = rotate(queries[:, :, NOPE:], cosine, sine_table).astype(jnp.bfloat16)
    softmax_scale = (NOPE + ROPE) ** (-0.5)
    grown = jnp.dot(compressed, w_expand, preferred_element_type=jnp.float32).astype(jnp.bfloat16)
    local_kv = grown.reshape(compressed.shape[0], local_heads, NOPE + VDIM).reshape(
        tok_rows, local_heads * (NOPE + VDIM)
    )
    flat_kv = lax.all_gather(local_kv, "seq", axis=0, tiled=True)
    rope_keys = lax.all_gather(key_rope, "seq", axis=0, tiled=True)
    key_seg = lax.all_gather(segment, "seq", axis=0, tiled=True)
    key_value = (lambda: flat_kv.reshape(flat_kv.shape[0], local_heads, NOPE + VDIM))()
    row_max = jnp.full((local_heads, tok_rows), -jnp.inf, jnp.float32)
    denom_sum = jnp.zeros((local_heads, tok_rows), jnp.float32)
    accum = jnp.zeros((local_heads, tok_rows, VDIM), jnp.float32)
    key_count = key_seg.shape[0]
    key_pos = jnp.arange(key_count, dtype=jnp.int32)
    scores = jnp.einsum(
        "qhd,khd->hqk", query_nope, key_value[:, :, :NOPE], preferred_element_type=jnp.float32
    )
    scores = scores + jnp.einsum(
        "qhd,kd->hqk", query_rope, rope_keys, preferred_element_type=jnp.float32
    )
    allowed = (segment[:, None] == key_seg[None, :]) & (key_pos[None, :] <= positions[:, None])
    scores = jnp.where(allowed[None], scores * softmax_scale, -jnp.inf)
    new_max = jnp.max(scores, axis=2)
    safe_max = jnp.where(new_max == -jnp.inf, 0.0, new_max)
    weights = jnp.exp(scores - safe_max[:, :, None])
    rescale = jnp.exp(row_max - safe_max)
    denom_sum = denom_sum * rescale + jnp.sum(weights, axis=2)
    accum = accum * rescale[:, :, None] + jnp.einsum(
        "hqk,khd->hqd",
        weights.astype(jnp.bfloat16),
        key_value[:, :, NOPE:],
        preferred_element_type=jnp.float32,
    )
    row_max, denom_sum, accum = (new_max, denom_sum, accum)
    head_mix = (accum / denom_sum[:, :, None]).astype(jnp.bfloat16)
    attn_part = jnp.einsum(
        "hqd,hde->qe",
        head_mix,
        w_out.reshape(local_heads, VDIM, D),
        preferred_element_type=jnp.float32,
    )
    attention = lax.psum(attn_part.astype(jnp.bfloat16), "head").astype(jnp.float32)
    residual = (residual_in + attention).astype(jnp.bfloat16)
    moe_in = rms_scale(residual.astype(jnp.float32), moe_gain).astype(jnp.bfloat16)
    seq_count = lax.axis_size("seq")
    experts = seq_count * w_gate.shape[0]
    capacity = min(tok_rows, tok_rows * TOPK * 5 // (4 * experts))
    flat_expert = routes.reshape(-1)
    flat_count = flat_expert.shape[0]
    onehot = (flat_expert[:, None] == jnp.arange(experts, dtype=jnp.int32)[None, :]).astype(
        jnp.int32
    )
    slot_rank = jnp.sum((jnp.cumsum(onehot, axis=0) - 1) * onehot, axis=1)
    slot_place = flat_expert * capacity + slot_rank
    source = (
        jnp.full((experts * capacity,), flat_count, jnp.int32)
        .at[slot_place]
        .set(jnp.arange(flat_count, dtype=jnp.int32))
    )
    moe_ext = jnp.concatenate([moe_in, jnp.zeros((1, D), jnp.bfloat16)], axis=0)
    outgoing = moe_ext[source // TOPK].reshape(experts, capacity, D)
    slot_items = lax.all_to_all(outgoing, "seq", split_axis=0, concat_axis=0, tiled=True)
    sources, slot_count, feat_width = slot_items.shape
    flat_rows = slot_items.reshape(sources * slot_count, feat_width)
    gate_proj = jnp.dot(flat_rows, w_gate[0], preferred_element_type=jnp.float32)
    up_proj = jnp.dot(flat_rows, w_up[0], preferred_element_type=jnp.float32)
    hidden = (jax.nn.silu(gate_proj) * up_proj).astype(jnp.bfloat16)
    partial_out = jnp.dot(hidden, w_down[0], preferred_element_type=jnp.float32).astype(
        jnp.bfloat16
    )
    returned = lax.all_to_all(
        partial_out.reshape(sources, slot_count, feat_width),
        "seq",
        split_axis=0,
        concat_axis=0,
        tiled=True,
    )
    picked = returned.reshape(experts * capacity, D)[slot_place].reshape(tok_rows, TOPK, D)
    moe_part = jnp.sum(picked.astype(jnp.float32) * gates[:, :, None], axis=1)
    moe_total = lax.psum(moe_part.astype(jnp.bfloat16), "head").astype(jnp.float32)
    hidden_out = (residual.astype(jnp.float32) + moe_total).astype(jnp.bfloat16)
    page_rows = jnp.concatenate([compressed, key_rope], axis=1).reshape(-1, PAGE * (LATENT + ROPE))
    slots_here = page_rows.shape[0] // lax.axis_size("head")
    wanted = head_index * slots_here + jnp.arange(slots_here, dtype=jnp.int32)
    select = (page_table[0][None, :] == wanted[:, None]).astype(jnp.bfloat16)
    latent_cache = jnp.dot(select, page_rows, preferred_element_type=jnp.float32).astype(
        jnp.bfloat16
    )
    return (hidden_out, latent_cache)


def solution(mesh):
    return jax.shard_map(
        local,
        mesh=mesh,
        in_specs=(
            P("seq", None),
            P(),
            P(None, "head"),
            P(None, "head"),
            P(),
            P(None, "head"),
            P("head", None),
            P(),
            P("seq", None, "head"),
            P("seq", None, "head"),
            P("seq", "head", None),
            P("seq", None),
            P("seq", None),
            P("seq"),
            P("seq", None),
        ),
        out_specs=(P("seq", None), P(("seq", "head"), None)),
        check_vma=False,
    )
```

profile of v0, /device:TPU:1, one launch (start us, length us, event | category | flops | bytes accessed | tf_op | source)
XLA Modules:
  0.0 759.7 jit_solution(4238097851218379535)
XLA Ops:
  7.3 1.4 fusion.33
  8.7 1.6 convolution_convert_fusion.2
  10.3 8.5 %all_gather.13 = bf16[128,576]{0,1:T(8,128)(2,1)S(1)} all-gather(bf16[128,144]{0,1:T(8,128)(2,1)S(1)} %convolution_convert_fusion.2), channel_id=1, replica_groups=mesh['seq'=64,'head'=4] {'head'}, dimensions={1}, use_global_device_ids=true | all-gather | bytes 184320 | tf_op jit(solution)/shard_map/all_gather | solution.py:74
  20.6 2.3 convolution_convert_fusion.1
  24.3 3.4 reduce-window.6
  28.0 154.9 %all-gather = s32[64,1,128]{2,1,0:T(1,128)S(1)} all-gather(s32[1,1,128]{2,1,0:T(1,128)S(1)} %bitcast.65), channel_id=1, replica_groups=mesh['seq'=64,'head'=4] {'seq'}, dimensions={0}, use_global_device_ids=true | all-gather | bytes 33280 | tf_op jit(solution)/shard_map/all_gather | solution.py:93
  182.9 2.4 fusion.57
  187.1 9.3 %fusion.41 = f32[8192,128,4]{0,1,2:T(8,128)} fusion(bf16[8192,64]{0,1:T(8,128)(2,1)} %all-gather.6.cloned.1.call-done, bf16[128,4,32]{0,2,1:T(8,128)(2,1)S(1)} %get-tuple-element.5, bf16[128,4,32]{0,2,1:T(8,128)(2,1)S(1)} %get-tuple-element.4), kind=kOutput, calls=%fused_computation.44 | convolution fusion | flops 537001984 | bytes 17891328 | tf_op jit(solution)/shard_map/qhd,kd->hqk/dot_general | solution.py:103
  196.4 119.5 %all-gather.4.cloned.1.call-done = bf16[8192,1024]{1,0:T(8,128)(2,1)} async-done(((bf16[128,1024]{1,0:T(8,128)(2,1)}), bf16[8192,1024]{1,0:T(8,128)(2,1)}) %all-gather.4.cloned.1.call-update) | async-done | bytes 16777232 | tf_op jit(solution)/shard_map/all_gather | solution.py:91
  315.8 27.9 %reshape.239 = bf16[8192,4,256]{2,1,0:T(4,128)(2,1)} reshape(bf16[8192,1024]{1,0:T(8,128)(2,1)} %all-gather.4.cloned.1.call-done) | data formatting | bytes 33554432 | tf_op jit(solution)/shard_map/reshape | solution.py:94
  343.7 15.7 %fusion.74 = (bf16[8192,4,128]{2,1,0:T(4,128)(2,1)}, bf16[8192,4,128]{2,1,0:T(4,128)(2,1)}) fusion(bf16[8192,4,256]{2,1,0:T(4,128)(2,1)} %reshape.239), kind=kLoop, calls=%fused_computation.102 | loop fusion | bytes 33554432 | tf_op jit(solution)/shard_map/slice | solution.py:101
  359.4 14.4 %fusion.75 = (f32[4,128]{1,0:T(4,128)S(1)}, f32[4,128,8192]{2,1,0:T(8,128)}) fusion(f32[8192,128,4]{0,1,2:T(8,128)} %fusion.41, bf16[8192,4,128]{2,1,0:T(4,128)(2,1)} %get-tuple-element.2, f32[128,4,192]{0,2,1:T(8,128)S(1)} %bitcast.61, pred[128,8192]{1,0:T(8,128)(4,1)S(1)} %fusion.9), kind=kOutput, calls=%fused_computation.103 | convolution fusion | flops 1090518528 | bytes 43124736 | tf_op jit(solution)/shard_map/qhd,khd->hqk/dot_general | solution.py:100
  373.8 8.3 %fusion.2 = f32[4,128]{1,0:T(4,128)S(1)} fusion(f32[4,128,8192]{2,1,0:T(8,128)} %get-tuple-element.15, f32[4,128]{1,0:T(4,128)S(1)} %compare_select_fusion.2), kind=kLoop, calls=%fused_computation.7 | loop fusion | flops 8388096 | bytes 16781312 | tf_op jit(solution)/shard_map/reduce_sum | solution.py:112
  382.1 12.9 %fusion.10 = bf16[128,2048]{1,0:T(8,128)(2,1)} fusion(bf16[4,128,2048]{2,1,0:T(8,128)(2,1)S(1)} %bitcast.59, bf16[8192,4,128]{2,1,0:T(4,128)(2,1)} %get-tuple-element.3, f32[4,128,8192]{2,1,0:T(8,128)} %get-tuple-element.15, f32[4,128]{1,0:T(4,128)S(1)} %compare_select_fusion.2, f32[4,128]{1,0:T(4,128)S(1)} %get-tuple-element.9, ...), kind=kOutput, calls=%fused_computation.18 | convolution fusion | flops 1351024640 | bytes 27793408 | tf_op jit(solution)/shard_map/hqd,hde->qe/dot_general | solution.py:121
  395.2 3.6 scatter_custom_fusion
  398.9 37.5 %all-reduce.4.cloned.1.call-done = bf16[128,2048]{1,0:T(8,128)(2,1)} async-done(((bf16[128,2048]{1,0:T(8,128)(2,1)}), bf16[128,2048]{1,0:T(8,128)(2,1)}) %all-reduce.4.cloned.1.call-update) | async-done | bytes 524304 | tf_op jit(solution)/shard_map/psum | solution.py:127
  436.4 1.3 fusion.37
  439.0 5.9 gather_fusion
  444.9 5.1 reshape.242
  450.0 107.4 %all_to_all.10 = bf16[64,15,2048]{2,1,0:T(8,128)(2,1)} all-to-all(bf16[64,15,2048]{2,1,0:T(8,128)(2,1)} %reshape.242), channel_id=1, replica_groups=mesh['seq'=64,'head'=4] {'seq'}, dimensions={0} | all-to-all | bytes 7864320 | tf_op jit(solution)/shard_map/all_to_all | solution.py:147
  557.5 5.2 reshape.243
  562.7 5.0 fusion.13
  567.7 8.7 %convolution_convert_fusion = bf16[960,2048]{1,0:T(8,128)(2,1)} fusion(bf16[1,352,2048]{2,1,0:T(8,128)(2,1)S(1)} %copy-done.12, bf16[960,2048]{1,0:T(8,128)(2,1)} %reshape.243, bf16[1,2048,352]{1,2,0:T(8,128)(2,1)} %param.24, f32[960,352]{0,1:T(8,128)} %fusion.13), kind=kOutput, calls=%fused_computation.16 | convolution fusion | flops 2772234240 | bytes 12099584 | tf_op jit(solution)/shard_map/dot_general | solution.py:153
  576.4 5.1 reshape.244
  581.5 8.0 %all-to-all-start.1 = ((bf16[64,15,2048]{2,1,0:T(8,128)(2,1)}), bf16[64,15,2048]{2,1,0:T(8,128)(2,1)}, u32[]{:S(2)}, u32[]{:S(2)}) async-start(bf16[64,15,2048]{2,1,0:T(8,128)(2,1)} %reshape.244), calls=%async_computation.1 | async-start | bytes 8388608 | tf_op jit(solution)/shard_map/all_to_all | solution.py:156
  590.0 91.7 %all-to-all-done.1 = bf16[64,15,2048]{2,1,0:T(8,128)(2,1)} async-done(((bf16[64,15,2048]{2,1,0:T(8,128)(2,1)}), bf16[64,15,2048]{2,1,0:T(8,128)(2,1)}, u32[]{:S(2)}, u32[]{:S(2)}) %all-to-all-start.1) | async-done | bytes 3932192 | tf_op jit(solution)/shard_map/all_to_all | solution.py:156
  681.7 5.1 reshape.245
  686.8 9.0 %gather_fusion.1 = bf16[768,2048]{1,0:T(8,128)(2,1)S(1)} fusion(bf16[960,2048]{1,0:T(8,128)(2,1)} %reshape.245, s32[1024]{0:T(1024)S(1)} %pad_clamp_fusion), kind=kCustom, calls=%fused_computation.1 | custom fusion | bytes 6294528 | tf_op jit(solution)/shard_map/gather | solution.py:163
  695.7 3.7 reshape.248
  699.5 7.5 multiply_reduce_fusion
  709.9 40.9 %all-reduce.6.cloned.1.call-done = bf16[128,2048]{1,0:T(8,128)(2,1)} async-done(((bf16[128,2048]{1,0:T(8,128)(2,1)}), bf16[128,2048]{1,0:T(8,128)(2,1)}) %all-reduce.6.cloned.1.call-update) | async-done | bytes 524304 | tf_op jit(solution)/shard_map/psum | solution.py:165
  750.8 2.4 fusion.40
  (76 shorter events, 10.0 us)
Async XLA Ops:
  7.2 175.8 %copy-start = (bf16[2048,768]{1,0:T(8,128)(2,1)S(1)}, bf16[2048,768]{1,0:T(8,128)(2,1)}, u32[]{:S(2)}) copy-start(bf16[2048,768]{1,0:T(8,128)(2,1)} %param.17) | copy-start | bytes 9437188
  7.2 175.8 %copy-start.7 = (f32[2048]{0:T(1024)S(1)}, f32[2048]{0:T(1024)}, u32[]{:S(2)}) copy-start(f32[2048]{0:T(1024)} %param.16) | copy-start | bytes 24580
  7.2 15.7 %copy-start.6 = (s32[128,6]{0,1:T(8,128)S(1)}, s32[128,6]{0,1:T(8,128)}, u32[]{:S(2)}) copy-start(s32[128,6]{0,1:T(8,128)} %param.26) | copy-start | bytes 9220
  7.2 20.8 %copy-start.10 = (s32[128]{0:T(128)S(1)}, s32[128]{0:T(128)}, u32[]{:S(2)}) copy-start(s32[128]{0:T(128)} %param.28) | copy-start | bytes 1540
  7.2 179.8 %all-gather.6.cloned.1.call-start = ((), (), s32[]{:S(2)}) async-start(), calls=%async_computation.3 | async-start | bytes 1064960 | tf_op jit(solution)/shard_map/all_gather | solution.py:92
  19.6 296.2 %all-gather.4.cloned.1.call-start = ((), (), s32[]{:S(2)}) async-start(), calls=%async_computation.2 | async-start | bytes 17039360 | tf_op jit(solution)/shard_map/all_gather | solution.py:91
  22.9 413.5 %all-reduce.4.cloned.1.call-start = ((), (), s32[]{:S(2)}) async-start(), calls=%async_computation.4 | async-start | bytes 1048576 | tf_op jit(solution)/shard_map/psum | solution.py:127
  185.4 0.7 copy-start.4
  343.7 15.7 %copy-start.5 = (f32[128,768]{0,1:T(8,128)S(1)}, f32[128,768]{0,1:T(8,128)}, u32[]{:S(2)}) copy-start(f32[128,768]{0,1:T(8,128)} %copy-done.4) | copy-start | bytes 1179652
  373.8 8.3 %copy-start.3 = (bf16[512,2048]{1,0:T(8,128)(2,1)S(1)}, bf16[512,2048]{1,0:T(8,128)(2,1)}, u32[]{:S(2)}) copy-start(bf16[512,2048]{1,0:T(8,128)(2,1)} %param.21) | copy-start | bytes 6291460
  382.1 54.2 %copy-start.2 = (bf16[128,2048]{1,0:T(8,128)(2,1)S(1)}, bf16[128,2048]{1,0:T(8,128)(2,1)}, u32[]{:S(2)}) copy-start(bf16[128,2048]{1,0:T(8,128)(2,1)} %param.15) | copy-start | bytes 1572868
  382.1 55.5 %copy-start.8 = (f32[2048]{0:T(1024)S(1)}, f32[2048]{0:T(1024)}, u32[]{:S(2)}) copy-start(f32[2048]{0:T(1024)} %param.22) | copy-start | bytes 24580
  557.5 5.2 copy-start.11
  562.7 5.0 copy-start.12
  581.5 8.3 %copy-start.9 = (f32[128,6]{0,1:T(8,128)S(1)}, f32[128,6]{0,1:T(8,128)}, u32[]{:S(2)}) copy-start(f32[128,6]{0,1:T(8,128)} %param.27) | copy-start | bytes 9220
  581.5 100.2 %all-to-all-start.1 = ((bf16[64,15,2048]{2,1,0:T(8,128)(2,1)}), bf16[64,15,2048]{2,1,0:T(8,128)(2,1)}, u32[]{:S(2)}, u32[]{:S(2)}) async-start(bf16[64,15,2048]{2,1,0:T(8,128)(2,1)} %reshape.244), calls=%async_computation.1 | async-start | bytes 8388608 | tf_op jit(solution)/shard_map/all_to_all | solution.py:156
  589.5 161.3 %all-reduce.6.cloned.1.call-start = ((), (), s32[]{:S(2)}) async-start(), calls=%async_computation.5 | async-start | bytes 1048576 | tf_op jit(solution)/shard_map/psum | solution.py:165
  699.5 9.5 %copy-start.13 = (s32[1,4]{1,0:T(1,128)S(1)}, s32[1,4]{1,0:T(1,128)}, u32[]{:S(2)}) copy-start(s32[1,4]{1,0:T(1,128)} %param.29) | copy-start | bytes 52
  699.5 53.7 %copy-start.1 = (bf16[2048,768]{1,0:T(8,128)(2,1)S(1)}, bf16[2048,768]{1,0:T(8,128)(2,1)}, u32[]{:S(2)}) copy-start(bf16[2048,768]{1,0:T(8,128)(2,1)} %param.17) | copy-start | bytes 9437188
Sparse Core Ops, SparseCore 0:
  19.7 91.4 all-gather.5
  114.8 201.0 all-gather.3
  395.2 41.0 all-reduce.3
  707.2 43.6 all-reduce.5
where the time goes:
time: 762 us; the launch traced here: 760 us
  waiting for transfers between devices  290 us (38%)
  blocking collectives  271 us (36%)
  local copies, waits for them, and re-layouts  90.1 us (12%)
  matrix products  56.9 us (7%)
  other arithmetic  29.8 us (4%)
  between operations  14.1 us (2%)
  starting transfers between devices  8.44 us (1%)
    all_gather x1, blocking collectives, local(): key_seg = lax.all_gather(segment, 'seq', axis=0, tiled=True)  155 us
    all_gather x1, waiting for transfers between devices, local(): flat_kv = lax.all_gather(local_kv, 'seq', axis=0, tiled=True)  119 us
    all_to_all x1, blocking collectives, local(): lax.all_to_all(outgoing, 'seq', split_axis=0, concat_axis=0, tiled=True)  107 us
    all_to_all x1, waiting for transfers between devices, local(): lax.all_to_all(partial_out.reshape(sources, slot_count, feat_width), 'seq...  91.7 us
    psum x1, waiting for transfers between devices, local(): lax.psum(moe_part.astype(jnp.bfloat16), 'head').astype(jnp.float32)  40.9 us
    psum x1, waiting for transfers between devices, local(): lax.psum(attn_part.astype(jnp.bfloat16), 'head').astype(jnp.float32)  37.5 us
    reshape x1, local copies, waits for them, and re-layouts, local(): flat_kv.reshape(flat_kv.shape[0], local_heads, NOPE + VDIM)  27.9 us
    slice x1, local copies, waits for them, and re-layouts, local(): key_value[:, :, :NOPE]  15.7 us
  transfers between devices with their start and end apart: 5, of which 4 were waited for; matrix products, arithmetic and copies ran while one was open for 4% of the time, Pallas kernels for 0%

commit v1 on v0

v1 whole, which is shorter than its diff:
```python
import functools

import jax
import jax.numpy as jnp
from jax import lax
from jax.experimental import pallas as pl
from jax.experimental.pallas import tpu as pltpu
from jax.sharding import PartitionSpec as P

D = 2048
NOPE = 128
ROPE = 64
VDIM = 128
LATENT = 512
TOPK = 6
PAGE = 32
LONGEST = 6144
SLOTS = 16
KT = 512

EPS = 1e-06
THETA = 50000.0
F32 = jnp.float32
BF16 = jnp.bfloat16


def rms_scale(values, scale_gain):
    mean_sq = jnp.mean(values * values, axis=-1, keepdims=True)
    return values * lax.rsqrt(mean_sq + EPS) * scale_gain


def rope_tables(positions, feat_width):
    half_width = feat_width // 2
    inv_freq = THETA ** (-jnp.arange(half_width, dtype=F32) * 2.0 / feat_width)
    angles = positions.astype(F32)[:, None] * inv_freq[None, :]
    return (jnp.cos(angles), jnp.sin(angles))


def rotate(values, cosine, sine_table):
    half_width = values.shape[-1] // 2
    table_shape = cosine.shape[:1] + (1,) * (values.ndim - 2) + cosine.shape[1:]
    cosine = cosine.reshape(table_shape)
    sine_table = sine_table.reshape(table_shape)
    lower_half = values[..., :half_width]
    upper_half = values[..., half_width:]
    return jnp.concatenate(
        [
            lower_half * cosine - upper_half * sine_table,
            upper_half * cosine + lower_half * sine_table,
        ],
        axis=-1,
    )


def dot(a, b):
    return jnp.dot(a, b, preferred_element_type=F32)


def attend_kernel(tok, heads, ql_ref, qr_ref, keys_ref, qseg_ref, kseg_ref, o_ref, m_ref, l_ref, acc_ref):
    s = lax.axis_index("seq")
    rows = heads * tok
    m_ref[...] = jnp.full_like(m_ref, -1e30)
    l_ref[...] = jnp.zeros_like(l_ref)
    acc_ref[...] = jnp.zeros_like(acc_ref)
    qpos = s * tok + lax.broadcasted_iota(jnp.int32, (rows, 1), 0) % tok
    first = jnp.maximum(s * tok - (LONGEST - 1), 0) // KT
    last = (s * tok + tok - 1) // KT + 1

    def step(kt, carry):
        at = pl.multiple_of(kt * KT, KT)
        c = keys_ref[pl.ds(at, KT), :LATENT]
        kr = keys_ref[pl.ds(at, KT), LATENT:]
        sc = lax.dot_general(ql_ref[...], c, (((1,), (1,)), ((), ())), preferred_element_type=F32)
        sc = sc + lax.dot_general(qr_ref[...], kr, (((1,), (1,)), ((), ())), preferred_element_type=F32)
        kpos = at + lax.broadcasted_iota(jnp.int32, (1, KT), 1)
        ok = (qseg_ref[...] == kseg_ref[kt]) & (kpos <= qpos)
        sc = jnp.where(ok, sc, -1e30)
        m_old = m_ref[...]
        m_new = jnp.maximum(m_old, jnp.max(sc, axis=1, keepdims=True))
        p = jnp.where(ok, jnp.exp(sc - m_new), 0.0)
        scale = jnp.exp(m_old - m_new)
        l_ref[...] = l_ref[...] * scale + jnp.sum(p, axis=1, keepdims=True)
        acc_ref[...] = acc_ref[...] * scale + dot(p.astype(BF16), c)
        m_ref[...] = m_new
        return carry

    lax.fori_loop(first, last, step, 0)
    o_ref[...] = (acc_ref[...] / l_ref[...]).astype(BF16)


def attend(ql, qr, keys, qseg, kseg, tok, heads):
    rows = heads * tok
    return pl.pallas_call(
        functools.partial(attend_kernel, tok, heads),
        out_shape=jax.ShapeDtypeStruct((rows, LATENT), BF16),
        in_specs=[pl.BlockSpec(memory_space=pltpu.VMEM)] * 5,
        out_specs=pl.BlockSpec(memory_space=pltpu.VMEM),
        scratch_shapes=[
            pltpu.VMEM((rows, 1), F32),
            pltpu.VMEM((rows, 1), F32),
            pltpu.VMEM((rows, LATENT), F32),
        ],
        compiler_params=pltpu.CompilerParams(vmem_limit_bytes=48 << 20),
    )(ql, qr, keys, qseg, kseg)


def local(
    hidden_in,
    attn_gain,
    w_query,
    w_latent,
    latent_gain,
    w_expand,
    w_out,
    moe_gain,
    w_gate,
    w_up,
    w_down,
    routes,
    gates,
    segment,
    page_table,
):
    tok = hidden_in.shape[0]
    heads = w_out.shape[0] // VDIM
    n_head = lax.axis_size("head")
    seq_index = lax.axis_index("seq")
    head_index = lax.axis_index("head")
    positions = seq_index * tok + jnp.arange(tok, dtype=jnp.int32)
    cosine, sine_table = rope_tables(positions, ROPE)
    residual_in = hidden_in.astype(F32)
    normed = rms_scale(residual_in, attn_gain).astype(BF16)
    latent_part = dot(normed, w_latent).astype(BF16)
    latent_raw = lax.all_gather(latent_part, "head", axis=1, tiled=True)
    compressed = rms_scale(latent_raw[:, :LATENT].astype(F32), latent_gain).astype(BF16)
    key_rope = rotate(latent_raw[:, LATENT:].astype(F32), cosine, sine_table).astype(BF16)
    latent = jnp.concatenate([compressed, key_rope], axis=1)
    part = tok // n_head
    mine = lax.dynamic_slice_in_dim(latent, head_index * part, part, 0)
    keys = lax.all_gather(mine, ("seq", "head"), axis=0, tiled=True)
    key_seg = lax.all_gather(segment, "seq", axis=0, tiled=True)

    scale = (NOPE + ROPE) ** (-0.5)
    queries = dot(normed, w_query).reshape(tok, heads, NOPE + ROPE)
    query_nope = queries[:, :, :NOPE].astype(BF16)
    query_rope = (rotate(queries[:, :, NOPE:], cosine, sine_table) * scale).astype(BF16)
    expand = w_expand.reshape(LATENT, heads, NOPE + VDIM)
    q_lat = jnp.einsum("qhd,chd->hqc", query_nope, expand[:, :, :NOPE], preferred_element_type=F32)
    q_lat = (q_lat * scale).astype(BF16).reshape(heads * tok, LATENT)
    q_rope = query_rope.transpose(1, 0, 2).reshape(heads * tok, ROPE)
    qseg = jnp.tile(segment, heads)[:, None]
    mixed = attend(q_lat, q_rope, keys, qseg, key_seg.reshape(-1, 1, KT), tok, heads)
    head_mix = jnp.einsum(
        "hqc,chd->qhd", mixed.reshape(heads, tok, LATENT), expand[:, :, NOPE:], preferred_element_type=F32
    ).astype(BF16)
    attn_part = dot(head_mix.reshape(tok, heads * VDIM), w_out).astype(BF16)
    attention = lax.psum_scatter(attn_part, "head", scatter_dimension=1, tiled=True).astype(F32)
    cols = D // n_head
    own_in = lax.dynamic_slice_in_dim(residual_in, head_index * cols, cols, 1)
    residual = (own_in + attention).astype(BF16)

    experts = lax.axis_size("seq")
    names = routes[:, :, None] == jnp.arange(experts, dtype=jnp.int32)
    picked = jnp.any(names, axis=1)
    gate_of = jnp.sum(jnp.where(names, gates[:, :, None], 0.0), axis=1)
    below = jnp.tril(jnp.ones((tok, tok), F32), -1)
    rank = dot(below.astype(BF16), picked.astype(BF16)).astype(jnp.int32)
    place = (rank.T[:, None, :] == jnp.arange(SLOTS, dtype=jnp.int32)[None, :, None]) & picked.T[:, None, :]
    send = place.astype(BF16).reshape(experts * SLOTS, tok)
    weight = jnp.where(place, gate_of.T[:, None, :], 0.0).reshape(experts * SLOTS, tok)
    outgoing = dot(send, residual).astype(BF16)
    items = lax.all_to_all(
        outgoing.reshape(experts, SLOTS, cols), "seq", split_axis=0, concat_axis=0, tiled=True
    ).reshape(experts * SLOTS, cols)
    rows = lax.all_gather(items, "head", axis=0)
    rows = rows.transpose(1, 0, 2).reshape(experts * SLOTS, D)
    moe_in = rms_scale(rows.astype(F32), moe_gain).astype(BF16)
    gate_proj = dot(moe_in, w_gate[0])
    up_proj = dot(moe_in, w_up[0])
    hidden = (jax.nn.silu(gate_proj) * up_proj).astype(BF16)
    partial_out = dot(hidden, w_down[0]).astype(BF16)
    total = lax.psum_scatter(partial_out, "head", scatter_dimension=1, tiled=True).astype(BF16)
    returned = lax.all_to_all(
        total.reshape(experts, SLOTS, cols), "seq", split_axis=0, concat_axis=0, tiled=True
    ).reshape(experts * SLOTS, cols)
    high = weight.astype(BF16)
    low = (weight - high.astype(F32)).astype(BF16)
    moe = lax.dot_general(high, returned, (((0,), (0,)), ((), ())), preferred_element_type=F32)
    moe = moe + lax.dot_general(low, returned, (((0,), (0,)), ((), ())), preferred_element_type=F32)
    out = (residual.astype(F32) + moe).astype(BF16)
    hidden_out = lax.all_gather(out, "head", axis=1, tiled=True)

    page_rows = latent.reshape(-1, PAGE * (LATENT + ROPE))
    slots_here = page_rows.shape[0] // n_head
    wanted = head_index * slots_here + jnp.arange(slots_here, dtype=jnp.int32)
    select = (page_table[0][None, :] == wanted[:, None]).astype(BF16)
    latent_cache = dot(select, page_rows).astype(BF16)
    return (hidden_out, latent_cache)


def solution(mesh):
    return jax.shard_map(
        local,
        mesh=mesh,
        in_specs=(
            P("seq", None),
            P(),
            P(None, "head"),
            P(None, "head"),
            P(),
            P(None, "head"),
            P("head", None),
            P(),
            P("seq", None, "head"),
            P("seq", None, "head"),
            P("seq", "head", None),
            P("seq", None),
            P("seq", None),
            P("seq"),
            P("seq", None),
        ),
        out_specs=(P("seq", None), P(("seq", "head"), None)),
        check_vma=False,
    )
```

time: 762 us -> 479 us (0.63)
  waiting for transfers between devices: 290 us -> 173 us
  local copies, waits for them, and re-layouts: 90.1 us -> 17.7 us
  blocking collectives: 271 us -> 219 us
  matrix products: 56.9 us -> 25 us
  other arithmetic: 29.8 us -> 9.88 us
    reduce_scatter x0 -> x2, waiting for transfers between devices: none -> 103 us  [the longest x1 53.8 us: local(): lax.psum_scatter(attn_part, 'head', scatter_dimension=1, tiled=True)]
    psum x2 -> x0, waiting for transfers between devices: 78.3 us -> none  [the longest x1 40.9 us: local(): lax.psum(moe_part.astype(jnp.bfloat16), 'head').astype(jnp.float32)]
    all_gather x2, waiting for transfers between devices: 119 us -> 45.6 us  [the longest x1 45.6 us: local(): rows = lax.all_gather(items, 'head', axis=0)]
    all_to_all x1, waiting for transfers between devices: 91.7 us -> 24.8 us  [local(): lax.all_to_all(total.reshape(experts, SLOTS, cols), 'seq', split_axis=0,...]
    all_to_all x1, blocking collectives: 107 us -> 40.9 us  [local(): lax.all_to_all(outgoing.reshape(experts, SLOTS, cols), 'seq', split_axis=...]
    reshape x6 -> x1, local copies, waits for them, and re-layouts: 48.6 us -> 0.89 us  [local(): page_rows = latent.reshape(-1, PAGE * (LATENT + ROPE))]
    dot_general x9 -> x12, matrix products: 56.9 us -> 25 us  [the longest x8 19.3 us: dot(): return jnp.dot(a, b, preferred_element_type=F32)]
    slice x2, local copies, waits for them, and re-layouts: 16 us -> 0.01 us  [the longest x1 0.01 us: local(): latent_raw[:, :LATENT].astype(F32)]
  transfers between devices with their start and end apart: 5 -> 5, of which waited for: 4 -> 4; matrix products, arithmetic and copies ran while one was open for 4% -> 3% of each run, Pallas kernels for 0% -> 0%
where the time goes in v1:
time: 479 us; the launch traced here: 478 us
  blocking collectives  219 us (46%)
  waiting for transfers between devices  173 us (36%)
  matrix products  25 us (5%)
  local copies, waits for them, and re-layouts  17.7 us (4%)
  between operations  14.1 us (3%)
  starting transfers between devices  12.9 us (3%)
  other arithmetic  9.88 us (2%)
  Pallas kernels  5.83 us (1%)
    all_gather x1, blocking collectives, local(): key_seg = lax.all_gather(segment, 'seq', axis=0, tiled=True)  160 us
    reduce_scatter x1, waiting for transfers between devices, local(): lax.psum_scatter(attn_part, 'head', scatter_dimension=1, tiled=True)  53.8 us
    reduce_scatter x1, waiting for transfers between devices, local(): lax.psum_scatter(partial_out, 'head', scatter_dimension=1, tiled=True)  48.7 us
    all_gather x1, waiting for transfers between devices, local(): rows = lax.all_gather(items, 'head', axis=0)  45.6 us
    all_to_all x1, blocking collectives, local(): lax.all_to_all(outgoing.reshape(experts, SLOTS, cols), 'seq', split_axis=...  40.9 us
    all_to_all x1, waiting for transfers between devices, local(): lax.all_to_all(total.reshape(experts, SLOTS, cols), 'seq', split_axis=0,...  24.8 us
    dot_general x8, matrix products, dot(): return jnp.dot(a, b, preferred_element_type=F32)  19.3 us
    all_to_all x1, starting transfers between devices, local(): lax.all_to_all(total.reshape(experts, SLOTS, cols), 'seq', split_axis=0,...  12.6 us
  transfers between devices with their start and end apart: 5, of which 4 were waited for; matrix products, arithmetic and copies ran while one was open for 3% of the time, Pallas kernels for 0%

profile of v1, /device:TPU:1, one launch (start us, length us, event | category | flops | bytes accessed | tf_op | source)
XLA Modules:
  0.0 477.8 jit_solution(17223021575968235349)
XLA Ops:
  7.2 1.4 multiply_reduce_fusion
  8.6 1.6 convolution_convert_fusion.4
  10.3 8.5 %all_gather.15 = bf16[128,576]{0,1:T(8,128)(2,1)S(1)} all-gather(bf16[128,144]{0,1:T(8,128)(2,1)S(1)} %convolution_convert_fusion.4), channel_id=1, replica_groups=mesh['seq'=64,'head'=4] {'head'}, dimensions={1}, use_global_device_ids=true | all-gather | bytes 184320 | tf_op jit(solution)/shard_map/all_gather | solution.py:134
  21.3 2.4 fusion.35
  23.8 0.7 copy-done.7
  24.6 2.3 copy.77
  27.0 160.2 %all-gather = s32[64,1,128]{2,1,0:T(1,128)} all-gather(s32[1,1,128]{2,1,0:T(1,128)S(1)} %bitcast.89), channel_id=1, replica_groups=mesh['seq'=64,'head'=4] {'seq'}, dimensions={0}, use_global_device_ids=true | all-gather | bytes 33280 | tf_op jit(solution)/shard_map/all_gather | solution.py:141
  187.3 2.3 fusion.10
  189.5 1.0 copy-done.1
  190.6 0.8 copy-done.2
  191.3 5.8 %shard_map.158 = bf16[512,512]{1,0:T(8,128)(2,1)S(1)} custom-call(bf16[512,512]{1,0:T(8,128)(2,1)S(1)} %bitcast.68, bf16[512,64]{1,0:T(8,128)(2,1)S(1)} %bitcast.69, bf16[8192,576]{1,0:T(8,128)(2,1)} %all-gather.4.cloned.1.call-done.keys_ref, s32[512,1]{1,0:T(8,128)S(1)} %copy.86.qseg_ref, s32[16,1,512]{2,1,0:T(1,128)S(1)} %bitcast.71), custom_call_target="tpu_custom_call" | custom-call | tf_op jit(solution)/shard_map/pallas_call | solution.py:93
  197.5 1.3 convolution_convert_fusion.1
  198.9 2.1 convert_element_type.109
  201.5 53.8 %reduce-scatter.3.cloned.1.call-done = bf16[128,512]{1,0:T(8,128)(2,1)} async-done(((bf16[128,2048]{1,0:T(8,128)(2,1)}), bf16[128,512]{1,0:T(8,128)(2,1)}) %reduce-scatter.3.cloned.1.call-update) | async-done | bytes 131088 | tf_op jit(solution)/shard_map/reduce_scatter | solution.py:157
  255.4 1.0 add_convert_fusion
  256.9 40.9 %all_to_all.10 = bf16[64,16,512]{2,1,0:T(8,128)(2,1)} all-to-all(bf16[64,16,512]{2,1,0:T(8,128)(2,1)S(1)} %bitcast.72), channel_id=1, replica_groups=mesh['seq'=64,'head'=4] {'seq'}, dimensions={0} | all-to-all | bytes 2097152 | tf_op jit(solution)/shard_map/all_to_all | solution.py:172
  298.1 45.6 %all-gather.6.cloned.1.call-done = bf16[4,1024,512]{2,1,0:T(8,128)(2,1)} async-done(((bf16[1,1024,512]{2,1,0:T(8,128)(2,1)}), bf16[4,1024,512]{2,1,0:T(8,128)(2,1)}) %all-gather.6.cloned.1.call-update) | async-done | bytes 4194320 | tf_op jit(solution)/shard_map/all_gather | solution.py:175
  343.7 6.3 %copy.87 = bf16[4,1024,512]{1,2,0:T(8,128)(2,1)} copy(bf16[4,1024,512]{2,1,0:T(8,128)(2,1)} %all-gather.6.cloned.1.call-done) | data formatting | bytes 8388608 | tf_op jit(solution)/shard_map/all_gather | solution.py:175
  350.0 3.3 fusion
  353.4 1.1 fusion.2
  354.5 2.0 copy-done.4
  356.5 2.9 fusion.5
  359.4 9.4 %convolution_convert_fusion = bf16[1024,2048]{1,0:T(8,128)(2,1)} fusion(bf16[1,352,2048]{2,1,0:T(8,128)(2,1)} %param.25, bf16[1024,2048]{0,1:T(8,128)(2,1)} %bitcast.74, bf16[1,2048,352]{1,2,0:T(8,128)(2,1)} %param.24, f32[1024,352]{0,1:T(8,128)} %fusion.5), kind=kOutput, calls=%fused_computation.5 | convolution fusion | flops 2957049856 | bytes 12713984 | tf_op jit(solution)/shard_map/dot_general | solution.py:56
  368.8 48.7 %reduce-scatter.5.cloned.1.call-done = bf16[1024,512]{1,0:T(8,128)(2,1)} async-done(((bf16[1024,2048]{1,0:T(8,128)(2,1)}), bf16[1024,512]{1,0:T(8,128)(2,1)}) %reduce-scatter.5.cloned.1.call-update) | async-done | bytes 1048592 | tf_op jit(solution)/shard_map/reduce_scatter | solution.py:182
  417.5 12.6 %all-to-all-start.1 = ((bf16[64,16,512]{2,1,0:T(8,128)(2,1)}), bf16[64,16,512]{2,1,0:T(8,128)(2,1)}, u32[]{:S(2)}, u32[]{:S(2)}) async-start(bf16[64,16,512]{2,1,0:T(8,128)(2,1)} %bitcast.80), calls=%async_computation.3 | async-start | bytes 2097152 | tf_op jit(solution)/shard_map/all_to_all | solution.py:183
  430.1 0.9 reshape.189
  431.0 1.1 fusion.41
  432.8 24.8 %all-to-all-done.1 = bf16[64,16,512]{2,1,0:T(8,128)(2,1)} async-done(((bf16[64,16,512]{2,1,0:T(8,128)(2,1)}), bf16[64,16,512]{2,1,0:T(8,128)(2,1)}, u32[]{:S(2)}, u32[]{:S(2)}) %all-to-all-start.1) | async-done | bytes 1048608 | tf_op jit(solution)/shard_map/all_to_all | solution.py:183
  457.6 1.6 convolution_bitcast_fusion
  459.2 1.6 fusion.13
  460.8 9.6 %all_gather.19 = bf16[128,2048]{1,0:T(8,128)(2,1)S(1)} all-gather(bf16[128,512]{1,0:T(8,128)(2,1)S(1)} %fusion.13), channel_id=1, replica_groups=mesh['seq'=64,'head'=4] {'head'}, dimensions={1}, use_global_device_ids=true | all-gather | bytes 655360 | tf_op jit(solution)/shard_map/all_gather | solution.py:191
  470.4 0.8 copy.96
  (75 shorter events, 5.2 us)
Async XLA Ops:
  7.2 14.1 %copy-start = (bf16[2048,768]{1,0:T(8,128)(2,1)S(1)}, bf16[2048,768]{1,0:T(8,128)(2,1)}, u32[]{:S(2)}) copy-start(bf16[2048,768]{1,0:T(8,128)(2,1)} %param.17) | copy-start | bytes 9437188
  7.2 14.1 %copy-start.11 = (f32[2048]{0:T(1024)S(1)}, f32[2048]{0:T(1024)}, u32[]{:S(2)}) copy-start(f32[2048]{0:T(1024)} %param.16) | copy-start | bytes 24580
  7.2 12.0 %copy-start.14 = (f32[512]{0:T(512)S(1)}, f32[512]{0:T(512)}, u32[]{:S(2)}) copy-start(f32[512]{0:T(512)} %param.19) | copy-start | bytes 6148
  7.2 182.3 %all-gather.4.cloned.1.call-start = ((), (), s32[]{:S(2)}) async-start(), calls=%async_computation.4 | async-start | bytes 10526720 | tf_op jit(solution)/shard_map/all_gather | solution.py:140
  19.8 0.7 copy-start.8
  21.1 234.3 %reduce-scatter.3.cloned.1.call-start = ((), (), s32[]{:S(2)}) async-start(), calls=%async_computation.5 | async-start | bytes 655360 | tf_op jit(solution)/shard_map/reduce_scatter | solution.py:157
  23.7 0.7 copy-start.7
  23.7 3.2 copy-start.15
  189.5 1.0 copy-start.1
  190.6 0.8 copy-start.2
  191.3 5.8 %copy-start.5 = (bf16[512,1024]{0,1:T(8,128)(2,1)S(1)}, bf16[512,1024]{0,1:T(8,128)(2,1)}, u32[]{:S(2)}) copy-start(bf16[512,1024]{0,1:T(8,128)(2,1)} %copy.77) | copy-start | bytes 3145732
  191.3 6.2 %copy-start.6 = (bf16[512,2048]{1,0:T(8,128)(2,1)S(1)}, bf16[512,2048]{1,0:T(8,128)(2,1)}, u32[]{:S(2)}) copy-start(bf16[512,2048]{1,0:T(8,128)(2,1)} %param.21) | copy-start | bytes 6291460
  197.5 3.6 copy-start.10
  198.8 144.9 %all-gather.6.cloned.1.call-start = ((), (), s32[]{:S(2)}) async-start(), calls=%async_computation.6 | async-start | bytes 5242880 | tf_op jit(solution)/shard_map/all_gather | solution.py:175
  256.4 41.6 %copy-start.12 = (f32[2048]{0:T(1024)S(1)}, f32[2048]{0:T(1024)}, u32[]{:S(2)}) copy-start(f32[2048]{0:T(1024)} %param.22) | copy-start | bytes 24580
  297.8 119.7 %reduce-scatter.5.cloned.1.call-start = ((), (), s32[]{:S(2)}) async-start(), calls=%async_computation.7 | async-start | bytes 5242880 | tf_op jit(solution)/shard_map/reduce_scatter | solution.py:182
  350.0 3.4 copy-start.3
  353.4 3.1 copy-start.16
  354.5 2.0 copy-start.4
  368.7 61.3 %copy-start.9 = (bf16[128,576]{1,0:T(8,128)(2,1)S(1)}, bf16[128,576]{1,0:T(8,128)(2,1)}, u32[]{:S(2)}) copy-start(bf16[128,576]{1,0:T(8,128)(2,1)} %copy-done.8) | copy-start | bytes 442372
  368.7 62.2 %copy-start.17 = (s32[1,4]{1,0:T(1,128)S(1)}, s32[1,4]{1,0:T(1,128)}, u32[]{:S(2)}) copy-start(s32[1,4]{1,0:T(1,128)} %param.29) | copy-start | bytes 52
  368.8 64.0 %copy-start.13 = (f32[128,6]{0,1:T(8,128)S(1)}, f32[128,6]{0,1:T(8,128)}, u32[]{:S(2)}) copy-start(f32[128,6]{0,1:T(8,128)} %param.27) | copy-start | bytes 9220
  417.5 40.1 %all-to-all-start.1 = ((bf16[64,16,512]{2,1,0:T(8,128)(2,1)}), bf16[64,16,512]{2,1,0:T(8,128)(2,1)}, u32[]{:S(2)}, u32[]{:S(2)}) async-start(bf16[64,16,512]{2,1,0:T(8,128)(2,1)} %bitcast.80), calls=%async_computation.3 | async-start | bytes 2097152 | tf_op jit(solution)/shard_map/all_to_all | solution.py:183
Sparse Core Ops, SparseCore 0:
  21.2 120.1 all-gather.3
  198.9 56.3 reduce-scatter.2
  297.9 45.6 all-gather.5
  368.9 48.5 reduce-scatter.4

commit v2 on v1

--- a/solution.py
+++ b/solution.py
@@ -17,6 +17,8 @@
 LONGEST = 6144
 SLOTS = 16
 KT = 512
+PART = 32
+WIDTH = 640
 
 EPS = 1e-06
 THETA = 50000.0
@@ -56,7 +58,123 @@
     return jnp.dot(a, b, preferred_element_type=F32)
 
 
-def attend_kernel(tok, heads, ql_ref, qr_ref, keys_ref, qseg_ref, kseg_ref, o_ref, m_ref, l_ref, acc_ref):
+def place_of():
+    seq, head = lax.axis_index("seq"), lax.axis_index("head")
+    return seq // 8, (seq // 2) % 4, (seq % 2) * 2 + head // 2, head % 2
+
+
+def device(z, x, y, core):
+    return (z * 8 + x * 2 + y // 2, (y % 2) * 2 + core)
+
+
+def remote(src, dst, send_sem, recv_sem, target):
+    return pltpu.make_async_remote_copy(
+        src_ref=src, dst_ref=dst, send_sem=send_sem, recv_sem=recv_sem,
+        device_id=target, device_id_type=pl.DeviceIdType.MESH,
+    )
+
+
+def gather_keys(mine_ref, keys, own_sem, zs, zr, ps, pr, cs, cr):
+    z, x, y, core = place_of()
+    partner = device(z, x, y, 1 - core)
+    up = lambda v: (v + 1) % 4
+    down = lambda v: (v + 3) % 4
+    z_peers = [device((z + d) % 8, x, y, core) for d in range(1, 8)]
+    x_peers = (device(z, up(x), y, core), device(z, down(x), y, core))
+    y_peers = (device(z, x, up(y), core), device(z, x, down(y), core))
+    barrier = pltpu.get_barrier_semaphore()
+    for peer in z_peers + list(x_peers) + list(y_peers) + [partner]:
+        pl.semaphore_signal(barrier, inc=1, device_id=peer, device_id_type=pl.DeviceIdType.MESH)
+    own = pltpu.make_async_copy(mine_ref, keys.at[z, x, y, core], own_sem)
+    own.start()
+    pl.semaphore_wait(barrier, 12)
+
+    z_sends = []
+    for d in (4, 3, 5, 2, 6, 1, 7):
+        copy = remote(mine_ref, keys.at[z, x, y, core], zs.at[d - 1], zr.at[d - 1], z_peers[d - 1])
+        copy.start()
+        z_sends.append(copy)
+    own.wait()
+    for d in range(1, 8):
+        there = keys.at[(z + 8 - d) % 8, x, y, core]
+        remote(there, there, zs.at[d - 1], zr.at[d - 1], partner).wait_recv()
+
+    def pieces(c, first):
+        def one(along, lo, n, step):
+            if along == "x":
+                return keys.at[pl.ds(lo, n), (x + step) % 4, y, c]
+            return keys.at[pl.ds(lo, n), x, (y + step) % 4, c]
+
+        def two(along, lo, n, step):
+            if along == "x":
+                return keys.at[pl.ds(lo, n), (x + step) % 4, :, c]
+            return keys.at[pl.ds(lo, n), :, (y + step) % 4, c]
+
+        other = "y" if first == "x" else "x"
+        out = [one(first, 0, 8, 0)]
+        for form, along in ((one, first), (two, other)):
+            out += [form(along, 0, 8, 3), form(along, 0, 8, 1), form(along, 0, 4, 2), form(along, 4, 4, 2)]
+        return out, one, two
+
+    def run(c, first):
+        mine, one, two = pieces(c, first)
+        theirs = pieces(1 - c, "y" if first == "x" else "x")[0]
+        sends = []
+
+        def share(i):
+            copy = remote(mine[i], mine[i], cs.at[i], cr.at[i], partner)
+            copy.start()
+            sends.append(copy)
+
+        share(0)
+        other = "y" if first == "x" else "x"
+        for ring, (form, along) in enumerate(((one, first), (two, other))):
+            right, left = x_peers if along == "x" else y_peers
+            base = 4 * ring
+
+            def push(k, region, target):
+                copy = remote(region, region, ps.at[base + k], pr.at[base + k], target)
+                copy.start()
+                sends.append(copy)
+
+            def arrive(k):
+                region = mine[1 + base + k]
+                remote(region, region, ps.at[base + k], pr.at[base + k], partner).wait_recv()
+
+            push(0, form(along, 0, 8, 0), right)
+            push(1, form(along, 0, 8, 0), left)
+            arrive(0)
+            push(2, form(along, 0, 4, 3), right)
+            share(1 + base)
+            arrive(1)
+            push(3, form(along, 4, 4, 1), left)
+            share(2 + base)
+            arrive(2)
+            share(3 + base)
+            arrive(3)
+            share(4 + base)
+        for i, region in enumerate(theirs):
+            remote(region, region, cs.at[i], cr.at[i], partner).wait_recv()
+        for copy in sends:
+            copy.wait_send()
+
+    @pl.when(core == 0)
+    def _():
+        run(0, "x")
+
+    @pl.when(core == 1)
+    def _():
+        run(1, "y")
+
+    for copy in z_sends:
+        copy.wait_send()
+
+
+def attend_kernel(
+    tok, heads, mine_ref, ql_ref, qr_ref, qseg_ref, o_ref,
+    keys, m_ref, l_ref, acc_ref, own_sem, zs, zr, ps, pr, cs, cr,
+):
+    gather_keys(mine_ref, keys, own_sem, zs, zr, ps, pr, cs, cr)
     s = lax.axis_index("seq")
     rows = heads * tok
     m_ref[...] = jnp.full_like(m_ref, -1e30)
@@ -67,13 +185,14 @@
     last = (s * tok + tok - 1) // KT + 1
 
     def step(kt, carry):
-        at = pl.multiple_of(kt * KT, KT)
-        c = keys_ref[pl.ds(at, KT), :LATENT]
-        kr = keys_ref[pl.ds(at, KT), LATENT:]
+        block = keys[kt // 2, pl.ds((kt % 2) * 2, 2)].reshape(KT, WIDTH)
+        c = block[:, :LATENT]
         sc = lax.dot_general(ql_ref[...], c, (((1,), (1,)), ((), ())), preferred_element_type=F32)
-        sc = sc + lax.dot_general(qr_ref[...], kr, (((1,), (1,)), ((), ())), preferred_element_type=F32)
-        kpos = at + lax.broadcasted_iota(jnp.int32, (1, KT), 1)
-        ok = (qseg_ref[...] == kseg_ref[kt]) & (kpos <= qpos)
+        more = lax.dot_general(qr_ref[...], block[:, LATENT:], (((1,), (1,)), ((), ())), preferred_element_type=F32)
+        sc = sc + more[:rows]
+        kseg = more[rows : rows + 1]
+        kpos = kt * KT + lax.broadcasted_iota(jnp.int32, (1, KT), 1)
+        ok = (qseg_ref[...] == kseg) & (kpos <= qpos)
         sc = jnp.where(ok, sc, -1e30)
         m_old = m_ref[...]
         m_new = jnp.maximum(m_old, jnp.max(sc, axis=1, keepdims=True))
@@ -88,20 +207,25 @@
     o_ref[...] = (acc_ref[...] / l_ref[...]).astype(BF16)
 
 
-def attend(ql, qr, keys, qseg, kseg, tok, heads):
+def attend(mine, ql, qr, qseg, tok, heads):
     rows = heads * tok
+    dma = pltpu.SemaphoreType.DMA
     return pl.pallas_call(
         functools.partial(attend_kernel, tok, heads),
         out_shape=jax.ShapeDtypeStruct((rows, LATENT), BF16),
-        in_specs=[pl.BlockSpec(memory_space=pltpu.VMEM)] * 5,
+        in_specs=[pl.BlockSpec(memory_space=pltpu.VMEM)] * 4,
         out_specs=pl.BlockSpec(memory_space=pltpu.VMEM),
         scratch_shapes=[
+            pltpu.VMEM((8, 4, 4, 2, PART, WIDTH), BF16),
             pltpu.VMEM((rows, 1), F32),
             pltpu.VMEM((rows, 1), F32),
             pltpu.VMEM((rows, LATENT), F32),
+            dma(()), dma((7,)), dma((7,)), dma((8,)), dma((8,)), dma((9,)), dma((9,)),
         ],
-        compiler_params=pltpu.CompilerParams(vmem_limit_bytes=48 << 20),
-    )(ql, qr, keys, qseg, kseg)
+        compiler_params=pltpu.CompilerParams(
+            collective_id=0, has_side_effects=True, vmem_limit_bytes=48 << 20
+        ),
+    )(mine, ql, qr, qseg)
 
 
 def local(
@@ -136,9 +260,10 @@
     key_rope = rotate(latent_raw[:, LATENT:].astype(F32), cosine, sine_table).astype(BF16)
     latent = jnp.concatenate([compressed, key_rope], axis=1)
     part = tok // n_head
-    mine = lax.dynamic_slice_in_dim(latent, head_index * part, part, 0)
-    keys = lax.all_gather(mine, ("seq", "head"), axis=0, tiled=True)
-    key_seg = lax.all_gather(segment, "seq", axis=0, tiled=True)
+    tagged = jnp.concatenate(
+        [latent, segment[:, None].astype(BF16), jnp.zeros((tok, WIDTH - LATENT - ROPE - 1), BF16)], axis=1
+    )
+    mine = lax.dynamic_slice_in_dim(tagged, head_index * part, part, 0)
 
     scale = (NOPE + ROPE) ** (-0.5)
     queries = dot(normed, w_query).reshape(tok, heads, NOPE + ROPE)
@@ -148,8 +273,16 @@
     q_lat = jnp.einsum("qhd,chd->hqc", query_nope, expand[:, :, :NOPE], preferred_element_type=F32)
     q_lat = (q_lat * scale).astype(BF16).reshape(heads * tok, LATENT)
     q_rope = query_rope.transpose(1, 0, 2).reshape(heads * tok, ROPE)
-    qseg = jnp.tile(segment, heads)[:, None]
-    mixed = attend(q_lat, q_rope, keys, qseg, key_seg.reshape(-1, 1, KT), tok, heads)
+    pick = (jnp.arange(WIDTH - LATENT) == ROPE).astype(BF16)
+    q_more = jnp.concatenate(
+        [
+            jnp.pad(q_rope, ((0, 0), (0, WIDTH - LATENT - ROPE))),
+            jnp.broadcast_to(pick[None, :], (16, WIDTH - LATENT)),
+        ],
+        axis=0,
+    )
+    qseg = jnp.tile(segment, heads)[:, None].astype(F32)
+    mixed = attend(mine, q_lat, q_more, qseg, tok, heads)
     head_mix = jnp.einsum(
         "hqc,chd->qhd", mixed.reshape(heads, tok, LATENT), expand[:, :, NOPE:], preferred_element_type=F32
     ).astype(BF16)

time: 479 us -> 361 us (0.75)
  blocking collectives: 219 us -> 59.1 us
  Pallas kernels: 5.83 us -> 59.2 us
  waiting for transfers between devices: 173 us -> 150 us
  local copies, waits for them, and re-layouts: 17.7 us -> 23.1 us
  other arithmetic: 9.88 us -> 15.2 us
    all_gather x1 -> x0, blocking collectives: 160 us -> none  [local(): key_seg = lax.all_gather(segment, 'seq', axis=0, tiled=True)]
    pallas_call x1, Pallas kernels: 5.83 us -> 59.2 us  [attend(): pl.pallas_call(functools.partial(attend_kernel, tok, heads), out_shape=ja...]
    reduce_scatter x1, waiting for transfers between devices: 53.8 us -> 32.9 us  [local(): lax.psum_scatter(attn_part, 'head', scatter_dimension=1, tiled=True)]
  transfers between devices with their start and end apart: 5 -> 4, of which waited for: 4 -> 4; matrix products, arithmetic and copies ran while one was open for 3% -> 2% of each run, Pallas kernels for 0% -> 0%
where the time goes in v2:
time: 361 us; the launch traced here: 360 us
  waiting for transfers between devices  150 us (42%)
  Pallas kernels  59.2 us (16%)
  blocking collectives  59.1 us (16%)
  matrix products  26.1 us (7%)
  local copies, waits for them, and re-layouts  23.1 us (6%)
  other arithmetic  15.2 us (4%)
  between operations  14.1 us (4%)
  starting transfers between devices  12.9 us (4%)
    pallas_call x1, Pallas kernels, attend(): pl.pallas_call(functools.partial(attend_kernel, tok, heads), out_shape=ja...  59.2 us
    reduce_scatter x1, waiting for transfers between devices, local(): lax.psum_scatter(partial_out, 'head', scatter_dimension=1, tiled=True)  48.7 us
    all_gather x1, waiting for transfers between devices, local(): rows = lax.all_gather(items, 'head', axis=0)  45.6 us
    all_to_all x1, blocking collectives, local(): lax.all_to_all(outgoing.reshape(experts, SLOTS, cols), 'seq', split_axis=...  41 us
    reduce_scatter x1, waiting for transfers between devices, local(): lax.psum_scatter(attn_part, 'head', scatter_dimension=1, tiled=True)  32.9 us
    all_to_all x1, waiting for transfers between devices, local(): lax.all_to_all(total.reshape(experts, SLOTS, cols), 'seq', split_axis=0,...  23.1 us
    dot_general x8, matrix products, dot(): return jnp.dot(a, b, preferred_element_type=F32)  19.3 us
    all_to_all x1, starting transfers between devices, local(): lax.all_to_all(total.reshape(experts, SLOTS, cols), 'seq', split_axis=0,...  12.6 us
  transfers between devices with their start and end apart: 4, of which 4 were waited for; matrix products, arithmetic and copies ran while one was open for 2% of the time, Pallas kernels for 0%

profile of v2, /device:TPU:1, one launch (start us, length us, event | category | flops | bytes accessed | tf_op | source)
XLA Modules:
  0.0 360.0 jit_solution(2043435277768294292)
XLA Ops:
  7.9 1.3 multiply_reduce_fusion
  9.2 1.6 convolution_convert_fusion.4
  10.9 8.5 %all_gather.9 = bf16[128,576]{0,1:T(8,128)(2,1)S(1)} all-gather(bf16[128,144]{0,1:T(8,128)(2,1)S(1)} %convolution_convert_fusion.4), channel_id=1, replica_groups=mesh['seq'=64,'head'=4] {'head'}, dimensions={1}, use_global_device_ids=true | all-gather | bytes 184320 | tf_op jit(solution)/shard_map/all_gather | solution.py:258
  24.2 2.4 fusion.36
  28.0 1.6 copy.91
  29.6 2.3 copy.86
  31.9 2.3 fusion.10
  34.2 1.4 fusion.26
  35.6 1.7 concatenate.17
  39.0 1.0 copy-done.1
  40.1 59.2 %shard_map.158 = bf16[512,512]{1,0:T(8,128)(2,1)S(1)} custom-call(bf16[32,640]{1,0:T(8,128)(2,1)S(1)} %constant_dynamic-slice_fusion.mine_ref, bf16[512,512]{1,0:T(8,128)(2,1)S(1)} %bitcast.68, bf16[528,128]{1,0:T(8,128)(2,1)S(1)} %fusion.37.qr_ref, f32[512,1]{1,0:T(8,128)S(1)} %copy.92.qseg_ref), custom_call_target="tpu_custom_call" | custom-call | tf_op jit(solution)/shard_map/pallas_call | solution.py:213
  99.3 1.3 convolution_convert_fusion.3
  100.6 1.3 convolution_convert_fusion.1
  102.0 2.1 convert_element_type.129
  104.7 32.9 %reduce-scatter.3.cloned.1.call-done = bf16[128,512]{1,0:T(8,128)(2,1)} async-done(((bf16[128,2048]{1,0:T(8,128)(2,1)}), bf16[128,512]{1,0:T(8,128)(2,1)}) %reduce-scatter.3.cloned.1.call-update) | async-done | bytes 131088 | tf_op jit(solution)/shard_map/reduce_scatter | solution.py:290
  137.5 1.0 add_convert_fusion
  139.0 41.0 %all_to_all.10 = bf16[64,16,512]{2,1,0:T(8,128)(2,1)} all-to-all(bf16[64,16,512]{2,1,0:T(8,128)(2,1)S(1)} %bitcast.70), channel_id=1, replica_groups=mesh['seq'=64,'head'=4] {'seq'}, dimensions={0} | all-to-all | bytes 2097152 | tf_op jit(solution)/shard_map/all_to_all | solution.py:305
  180.3 45.6 %all-gather.2.cloned.1.call-done = bf16[4,1024,512]{2,1,0:T(8,128)(2,1)} async-done(((bf16[1,1024,512]{2,1,0:T(8,128)(2,1)}), bf16[4,1024,512]{2,1,0:T(8,128)(2,1)}) %all-gather.2.cloned.1.call-update) | async-done | bytes 4194320 | tf_op jit(solution)/shard_map/all_gather | solution.py:308
  225.8 6.3 %copy.93 = bf16[4,1024,512]{1,2,0:T(8,128)(2,1)} copy(bf16[4,1024,512]{2,1,0:T(8,128)(2,1)} %all-gather.2.cloned.1.call-done) | data formatting | bytes 8388608 | tf_op jit(solution)/shard_map/all_gather | solution.py:308
  232.2 3.3 fusion
  235.6 1.1 fusion.2
  236.7 2.0 copy-done.3
  238.7 2.9 fusion.5
  241.5 9.4 %convolution_convert_fusion = bf16[1024,2048]{1,0:T(8,128)(2,1)} fusion(bf16[1,352,2048]{2,1,0:T(8,128)(2,1)} %param.25, bf16[1024,2048]{0,1:T(8,128)(2,1)} %bitcast.72, bf16[1,2048,352]{1,2,0:T(8,128)(2,1)} %param.24, f32[1024,352]{0,1:T(8,128)} %fusion.5), kind=kOutput, calls=%fused_computation.5 | convolution fusion | flops 2957049856 | bytes 12713984 | tf_op jit(solution)/shard_map/dot_general | solution.py:58
  251.0 48.7 %reduce-scatter.5.cloned.1.call-done = bf16[1024,512]{1,0:T(8,128)(2,1)} async-done(((bf16[1024,2048]{1,0:T(8,128)(2,1)}), bf16[1024,512]{1,0:T(8,128)(2,1)}) %reduce-scatter.5.cloned.1.call-update) | async-done | bytes 1048592 | tf_op jit(solution)/shard_map/reduce_scatter | solution.py:315
  299.7 12.6 %all-to-all-start.1 = ((bf16[64,16,512]{2,1,0:T(8,128)(2,1)}), bf16[64,16,512]{2,1,0:T(8,128)(2,1)}, u32[]{:S(2)}, u32[]{:S(2)}) async-start(bf16[64,16,512]{2,1,0:T(8,128)(2,1)} %bitcast.78), calls=%async_computation.3 | async-start | bytes 2097152 | tf_op jit(solution)/shard_map/all_to_all | solution.py:316
  313.0 1.8 reshape.204
  314.8 1.1 fusion.43
  316.7 23.1 %all-to-all-done.1 = bf16[64,16,512]{2,1,0:T(8,128)(2,1)} async-done(((bf16[64,16,512]{2,1,0:T(8,128)(2,1)}), bf16[64,16,512]{2,1,0:T(8,128)(2,1)}, u32[]{:S(2)}, u32[]{:S(2)}) %all-to-all-start.1) | async-done | bytes 1048608 | tf_op jit(solution)/shard_map/all_to_all | solution.py:316
  339.8 1.6 convolution_bitcast_fusion
  341.4 1.6 fusion.13
  343.0 9.6 %all_gather.11 = bf16[128,2048]{1,0:T(8,128)(2,1)S(1)} all-gather(bf16[128,512]{1,0:T(8,128)(2,1)S(1)} %fusion.13), channel_id=1, replica_groups=mesh['seq'=64,'head'=4] {'head'}, dimensions={1}, use_global_device_ids=true | all-gather | bytes 655360 | tf_op jit(solution)/shard_map/all_gather | solution.py:324
  (78 shorter events, 12.3 us)
Async XLA Ops:
  7.2 17.0 %copy-start = (bf16[2048,768]{1,0:T(8,128)(2,1)S(1)}, bf16[2048,768]{1,0:T(8,128)(2,1)}, u32[]{:S(2)}) copy-start(bf16[2048,768]{1,0:T(8,128)(2,1)} %param.17) | copy-start | bytes 9437188
  7.2 12.2 %copy-start.16 = (s32[128]{0:T(128)S(1)}, s32[128]{0:T(128)}, u32[]{:S(2)}) copy-start(s32[128]{0:T(128)} %param.28) | copy-start | bytes 1540
  7.2 130.4 %reduce-scatter.3.cloned.1.call-start = ((), (), s32[]{:S(2)}) async-start(), calls=%async_computation.4 | async-start | bytes 655360 | tf_op jit(solution)/shard_map/reduce_scatter | solution.py:290
  9.2 10.2 %copy-start.13 = (f32[128]{0:T(128)}, f32[128]{0:T(128)S(1)}, u32[]{:S(2)}) copy-start(f32[128]{0:T(128)S(1)} %add_rsqrt_fusion.2) | copy-start | bytes 1540
  24.1 3.2 copy-start.9
  26.6 0.8 copy-start.5
  29.6 8.4 %copy-start.14 = (bf16[128]{0:T(256)(128)(2,1)S(1)}, bf16[128]{0:T(256)(128)(2,1)}, u32[]{:S(2)}) copy-start(bf16[128]{0:T(256)(128)(2,1)} %compare_convert_fusion) | copy-start | bytes 772
  39.0 1.0 copy-start.1
  40.1 60.6 %copy-start.4 = (bf16[512,2048]{1,0:T(8,128)(2,1)S(1)}, bf16[512,2048]{1,0:T(8,128)(2,1)}, u32[]{:S(2)}) copy-start(bf16[512,2048]{1,0:T(8,128)(2,1)} %param.21) | copy-start | bytes 6291460
  100.6 3.6 copy-start.10
  101.9 123.9 %all-gather.2.cloned.1.call-start = ((), (), s32[]{:S(2)}) async-start(), calls=%async_computation.5 | async-start | bytes 5242880 | tf_op jit(solution)/shard_map/all_gather | solution.py:308
  138.6 41.7 %copy-start.11 = (f32[2048]{0:T(1024)S(1)}, f32[2048]{0:T(1024)}, u32[]{:S(2)}) copy-start(f32[2048]{0:T(1024)} %param.22) | copy-start | bytes 24580
  180.0 119.7 %reduce-scatter.5.cloned.1.call-start = ((), (), s32[]{:S(2)}) async-start(), calls=%async_computation.6 | async-start | bytes 5242880 | tf_op jit(solution)/shard_map/reduce_scatter | solution.py:315
  232.2 3.4 copy-start.2
  235.6 3.1 copy-start.15
  236.7 2.0 copy-start.3
  250.9 61.3 %copy-start.6 = (bf16[128,512]{1,0:T(8,128)(2,1)S(1)}, bf16[128,512]{1,0:T(8,128)(2,1)}, u32[]{:S(2)}) copy-start(bf16[128,512]{1,0:T(8,128)(2,1)} %fusion.26) | copy-start | bytes 393220
  250.9 61.3 %copy-start.7 = (bf16[128,32]{1,0:T(8,128)(2,1)S(1)}, bf16[128,32]{1,0:T(8,128)(2,1)}, u32[]{:S(2)}) copy-start(bf16[128,32]{1,0:T(8,128)(2,1)} %get-tuple-element.8) | copy-start | bytes 24580
  250.9 61.3 %copy-start.8 = (bf16[128,32]{1,0:T(8,128)(2,1)S(1)}, bf16[128,32]{1,0:T(8,128)(2,1)}, u32[]{:S(2)}) copy-start(bf16[128,32]{1,0:T(8,128)(2,1)} %get-tuple-element.9) | copy-start | bytes 24580
  250.9 63.9 %copy-start.17 = (s32[1,4]{1,0:T(1,128)S(1)}, s32[1,4]{1,0:T(1,128)}, u32[]{:S(2)}) copy-start(s32[1,4]{1,0:T(1,128)} %param.29) | copy-start | bytes 52
  251.0 65.7 %copy-start.12 = (f32[128,6]{0,1:T(8,128)S(1)}, f32[128,6]{0,1:T(8,128)}, u32[]{:S(2)}) copy-start(f32[128,6]{0,1:T(8,128)} %param.27) | copy-start | bytes 9220
  299.7 40.1 %all-to-all-start.1 = ((bf16[64,16,512]{2,1,0:T(8,128)(2,1)}), bf16[64,16,512]{2,1,0:T(8,128)(2,1)}, u32[]{:S(2)}, u32[]{:S(2)}) async-start(bf16[64,16,512]{2,1,0:T(8,128)(2,1)} %bitcast.78), calls=%async_computation.3 | async-start | bytes 2097152 | tf_op jit(solution)/shard_map/all_to_all | solution.py:316
Sparse Core Ops, SparseCore 0:
  102.1 35.4 reduce-scatter.2
  180.1 45.6 all-gather.1
  251.0 48.6 reduce-scatter.4

commit v3 on v2

--- a/solution.py
+++ b/solution.py
@@ -226,6 +226,252 @@
             collective_id=0, has_side_effects=True, vmem_limit_bytes=48 << 20
         ),
     )(mine, ql, qr, qseg)
+
+
+ORDER = ((0, 1), (7, 2), (6, 3), (5, 4))
+
+
+def experts_kernel(
+    mixed_ref, expand_ref, wout_ref, own_ref, pick_ref, high_ref, low_ref, gain_ref, wg_hbm, wu_hbm, wd_hbm, o_ref,
+    mix, apart, ain, res, outgoing, items, xin, wg, wu, wd, pout, cin, ysend, yin, back, ret, acc, fin,
+    w_sem, own_sem, rs, rr, a0s, a0r, as_, ar, fys, fyr, fps, fpr, fqs, fqr, xs, xr, ys, yr, b0s, b0r, bs, br, es, er,
+):
+    z, x, y, core = place_of()
+    seq, head = lax.axis_index("seq"), lax.axis_index("head")
+    yl = head // 2
+    here = seq % 8
+    partner = (seq, yl * 2 + 1 - core)
+    across = (seq, (1 - yl) * 2 + core)
+    q_partner = yl * 2 + 1 - core
+    q_across = (1 - yl) * 2 + core
+    q_far = (1 - yl) * 2 + 1 - core
+    tok = mix.shape[0]
+    mesh_id = pl.DeviceIdType.MESH
+
+    loads = [
+        pltpu.make_async_copy(src.at[0], dst, w_sem.at[i])
+        for i, (src, dst) in enumerate(((wg_hbm, wg), (wu_hbm, wu), (wd_hbm, wd)))
+    ]
+    for copy in loads:
+        copy.start()
+
+    barrier = pltpu.get_barrier_semaphore()
+
+    def greet(k, carry):
+        pl.semaphore_signal(barrier, inc=1, device_id=((seq + k) % 64, head), device_id_type=mesh_id)
+        return carry
+
+    lax.fori_loop(1, 64, greet, 0)
+    for d in range(1, 4):
+        pl.semaphore_signal(barrier, inc=1, device_id=(seq, (head + d) % 4), device_id_type=mesh_id)
+
+    heads = mixed_ref.shape[0] // tok
+    for h in range(heads):
+        value = expand_ref[:, h * (NOPE + VDIM) + NOPE : (h + 1) * (NOPE + VDIM)]
+        mix[:, h * VDIM : (h + 1) * VDIM] = dot(mixed_ref[h * tok : (h + 1) * tok, :], value).astype(BF16)
+    for q in range(4):
+        apart[q] = dot(mix[...], wout_ref[:, q * 512 : (q + 1) * 512]).astype(BF16)
+
+    pl.semaphore_wait(barrier, 66)
+
+    sends = []
+
+    def push(src, dst, send_sem, recv_sem, target):
+        copy = remote(src, dst, send_sem, recv_sem, target)
+        copy.start()
+        sends.append(copy)
+
+    def arrive(region, recv_sem):
+        remote(region, region, own_sem.at[2], recv_sem, partner).wait_recv()
+
+    for d in range(1, 4):
+        q = (head + d) % 4
+        push(apart.at[q], ain.at[d - 1], rs.at[d - 1], rr.at[d - 1], (seq, q))
+    total = apart[head].astype(F32)
+    for d in range(1, 4):
+        arrive(ain.at[d - 1], rr.at[d - 1])
+        total = total + ain[d - 1].astype(F32)
+    res[...] = (own_ref[...].astype(F32) + total).astype(BF16)
+
+    locals_ = []
+    for ja, jb in ORDER:
+        for j in (ja, jb):
+            zt = (z + j) % 8
+            outgoing[zt] = dot(pick_ref[zt], res[...]).astype(BF16).reshape(8, SLOTS, 512)
+            if j == 0:
+                copy = pltpu.make_async_copy(outgoing.at[z, here], items.at[head, z, here], own_sem.at[0])
+                copy.start()
+                locals_.append(copy)
+                for k in range(1, 8):
+                    to = (here + k) % 8
+                    push(
+                        outgoing.at[z, to], items.at[head, z, here], a0s.at[k - 1], a0r.at[k - 1], (z * 8 + to, head)
+                    )
+            else:
+
+                def send(i, carry, zt=zt, j=j):
+                    remote(
+                        outgoing.at[zt, i], items.at[head, z, here], as_.at[j], ar.at[j], (zt * 8 + i, head)
+                    ).start()
+                    return carry
+
+                lax.fori_loop(0, 8, send, 0)
+
+    def stage_a(g):
+        for j in ORDER[g]:
+            zs = (z + 8 - j) % 8
+            slab = items.at[head, zs]
+            if j == 0:
+                locals_[0].wait()
+                for k in range(1, 8):
+                    arrive(items.at[head, z, (here + 8 - k) % 8], a0r.at[k - 1])
+            else:
+                arrive(slab, ar.at[j])
+            push(slab, slab, fys.at[j], fyr.at[j], across)
+            push(slab, slab, fps.at[j], fpr.at[j], partner)
+
+    def stage_b(g):
+        for j in ORDER[g]:
+            slab = items.at[q_across, (z + 8 - j) % 8]
+            arrive(slab, fyr.at[j])
+            push(slab, slab, fqs.at[j], fqr.at[j], partner)
+
+    def stage_c(g):
+        if g == 0:
+            for copy in loads:
+                copy.wait()
+        for t, j in enumerate(ORDER[g]):
+            zs = (z + 8 - j) % 8
+            arrive(items.at[q_partner, zs], fpr.at[j])
+            arrive(items.at[q_far, zs], fqr.at[j])
+            mean_sq = jnp.zeros((tok, 1), F32)
+            for q in range(4):
+                v = items[q, zs].reshape(tok, 512).astype(F32)
+                mean_sq = mean_sq + jnp.sum(v * v, axis=1, keepdims=True)
+            inv = lax.rsqrt(mean_sq * (1.0 / D) + EPS)
+            for q in range(4):
+                v = items[q, zs].reshape(tok, 512).astype(F32)
+                cols = slice(q * 512, (q + 1) * 512)
+                xin[t * tok : (t + 1) * tok, cols] = (v * inv * gain_ref[:, cols]).astype(BF16)
+        gate = dot(xin[...], wg[...])
+        up = dot(xin[...], wu[...])
+        hidden = (gate / (1.0 + jnp.exp(-gate)) * up).astype(BF16)
+        for q in range(4):
+            part = dot(hidden, wd[:, q * 512 : (q + 1) * 512]).astype(BF16)
+            for t, j in enumerate(ORDER[g]):
+                pout[q, (z + 8 - j) % 8] = part[t * tok : (t + 1) * tok].reshape(8, SLOTS, 512)
+        for j in ORDER[g]:
+            zs = (z + 8 - j) % 8
+            for side in range(2):
+                push(
+                    pout.at[side * 2 + 1 - core, zs], cin.at[side, zs], xs.at[side, j], xr.at[side, j], partner
+                )
+
+    def stage_d(g):
+        for j in ORDER[g]:
+            zs = (z + 8 - j) % 8
+            for side in range(2):
+                arrive(cin.at[side, zs], xr.at[side, j])
+            ysend[zs] = (pout[q_across, zs].astype(F32) + cin[1 - yl, zs].astype(F32)).astype(BF16)
+            push(ysend.at[zs], yin.at[zs], ys.at[j], yr.at[j], across)
+
+    def stage_e(g):
+        for j in ORDER[g]:
+            zs = (z + 8 - j) % 8
+            arrive(yin.at[zs], yr.at[j])
+            both = pout[head, zs].astype(F32) + cin[yl, zs].astype(F32)
+            back[zs] = (both + yin[zs].astype(F32)).astype(BF16)
+            if j == 0:
+                copy = pltpu.make_async_copy(back.at[z, here], ret.at[z, here], own_sem.at[1])
+                copy.start()
+                locals_.append(copy)
+                for k in range(1, 8):
+                    to = (here + k) % 8
+                    push(back.at[z, to], ret.at[z, here], b0s.at[k - 1], b0r.at[k - 1], (z * 8 + to, head))
+            else:
+
+                def send(i, carry, zs=zs, j=j):
+                    remote(back.at[zs, i], ret.at[z, here], bs.at[j], br.at[j], (zs * 8 + i, head)).start()
+                    return carry
+
+                lax.fori_loop(0, 8, send, 0)
+
+    a, b, c, d, e = stage_a, stage_b, stage_c, stage_d, stage_e
+    for stage, g in (
+        (a, 0), (b, 0), (a, 1), (c, 0), (b, 1), (d, 0), (a, 2), (c, 1), (e, 0), (b, 2),
+        (d, 1), (a, 3), (c, 2), (e, 1), (b, 3), (d, 2), (c, 3), (e, 2), (d, 3), (e, 3),
+    ):
+        stage(g)
+
+    acc[...] = res[...].astype(F32)
+    for ja, jb in ORDER:
+        for j in (ja, jb):
+            ze = (z + j) % 8
+            if j == 0:
+                locals_[1].wait()
+                for k in range(1, 8):
+                    arrive(ret.at[z, (here + 8 - k) % 8], b0r.at[k - 1])
+            else:
+                arrive(ret.at[ze], br.at[j])
+            got = ret[ze].reshape(tok, 512)
+            acc[...] += dot(high_ref[ze], got) + dot(low_ref[ze], got)
+    fin[head] = acc[...].astype(BF16)
+    push(fin.at[head], fin.at[head], es.at[0], er.at[0], across)
+    push(fin.at[head], fin.at[head], es.at[1], er.at[1], partner)
+    arrive(fin.at[q_across], er.at[0])
+    push(fin.at[q_across], fin.at[q_across], es.at[2], er.at[2], partner)
+    arrive(fin.at[q_partner], er.at[1])
+    arrive(fin.at[q_far], er.at[2])
+    for q in range(4):
+        o_ref[:, q * 512 : (q + 1) * 512] = fin[q]
+    for copy in sends:
+        copy.wait_send()
+    for j in range(1, 8):
+        slab = outgoing.at[(z + j) % 8]
+        remote(slab, slab, as_.at[j], ar.at[j], partner).wait_send()
+        slab = back.at[(z + 8 - j) % 8]
+        remote(slab, slab, bs.at[j], br.at[j], partner).wait_send()
+
+
+def run_experts(mixed, expand, w_out, own_in, pick, high, low, gain, w_gate, w_up, w_down, tok):
+    dma = pltpu.SemaphoreType.DMA
+    vmem, hbm = pl.BlockSpec(memory_space=pltpu.VMEM), pl.BlockSpec(memory_space=pl.ANY)
+    ff = w_gate.shape[2]
+    rows = (8, 8, SLOTS, 512)
+    quarter = (tok, 512)
+    eight = [dma((8,))] * 2
+    return pl.pallas_call(
+        experts_kernel,
+        out_shape=jax.ShapeDtypeStruct((tok, D), BF16),
+        in_specs=[vmem] * 8 + [hbm] * 3,
+        out_specs=vmem,
+        scratch_shapes=[
+            pltpu.VMEM((tok, 512), BF16),
+            pltpu.VMEM((4,) + quarter, BF16),
+            pltpu.VMEM((3,) + quarter, BF16),
+            pltpu.VMEM(quarter, BF16),
+            pltpu.VMEM(rows, BF16),
+            pltpu.VMEM((4,) + rows, BF16),
+            pltpu.VMEM((2 * tok, D), BF16),
+            pltpu.VMEM((D, ff), BF16),
+            pltpu.VMEM((D, ff), BF16),
+            pltpu.VMEM((ff, D), BF16),
+            pltpu.VMEM((4,) + rows, BF16),
+            pltpu.VMEM((2,) + rows, BF16),
+            pltpu.VMEM(rows, BF16),
+            pltpu.VMEM(rows, BF16),
+            pltpu.VMEM(rows, BF16),
+            pltpu.VMEM(rows, BF16),
+            pltpu.VMEM(quarter, F32),
+            pltpu.VMEM((4,) + quarter, BF16),
+            dma((3,)), dma((3,)), dma((3,)), dma((3,)), dma((7,)), dma((7,)),
+            *eight, *eight, *eight, *eight,
+            dma((2, 8)), dma((2, 8)), *eight, dma((7,)), dma((7,)), *eight, dma((3,)), dma((3,)),
+        ],
+        compiler_params=pltpu.CompilerParams(
+            collective_id=1, has_side_effects=True, vmem_limit_bytes=56 << 20
+        ),
+    )(mixed, expand, w_out, own_in, pick, high, low, gain, w_gate, w_up, w_down)
 
 
 def local(
@@ -283,45 +529,27 @@
     )
     qseg = jnp.tile(segment, heads)[:, None].astype(F32)
     mixed = attend(mine, q_lat, q_more, qseg, tok, heads)
-    head_mix = jnp.einsum(
-        "hqc,chd->qhd", mixed.reshape(heads, tok, LATENT), expand[:, :, NOPE:], preferred_element_type=F32
-    ).astype(BF16)
-    attn_part = dot(head_mix.reshape(tok, heads * VDIM), w_out).astype(BF16)
-    attention = lax.psum_scatter(attn_part, "head", scatter_dimension=1, tiled=True).astype(F32)
     cols = D // n_head
-    own_in = lax.dynamic_slice_in_dim(residual_in, head_index * cols, cols, 1)
-    residual = (own_in + attention).astype(BF16)
-
+    own_in = lax.dynamic_slice_in_dim(hidden_in, head_index * cols, cols, 1)
     experts = lax.axis_size("seq")
     names = routes[:, :, None] == jnp.arange(experts, dtype=jnp.int32)
     picked = jnp.any(names, axis=1)
     gate_of = jnp.sum(jnp.where(names, gates[:, :, None], 0.0), axis=1)
     below = jnp.tril(jnp.ones((tok, tok), F32), -1)
     rank = dot(below.astype(BF16), picked.astype(BF16)).astype(jnp.int32)
-    place = (rank.T[:, None, :] == jnp.arange(SLOTS, dtype=jnp.int32)[None, :, None]) & picked.T[:, None, :]
-    send = place.astype(BF16).reshape(experts * SLOTS, tok)
-    weight = jnp.where(place, gate_of.T[:, None, :], 0.0).reshape(experts * SLOTS, tok)
-    outgoing = dot(send, residual).astype(BF16)
-    items = lax.all_to_all(
-        outgoing.reshape(experts, SLOTS, cols), "seq", split_axis=0, concat_axis=0, tiled=True
-    ).reshape(experts * SLOTS, cols)
-    rows = lax.all_gather(items, "head", axis=0)
-    rows = rows.transpose(1, 0, 2).reshape(experts * SLOTS, D)
-    moe_in = rms_scale(rows.astype(F32), moe_gain).astype(BF16)
-    gate_proj = dot(moe_in, w_gate[0])
-    up_proj = dot(moe_in, w_up[0])
-    hidden = (jax.nn.silu(gate_proj) * up_proj).astype(BF16)
-    partial_out = dot(hidden, w_down[0]).astype(BF16)
-    total = lax.psum_scatter(partial_out, "head", scatter_dimension=1, tiled=True).astype(BF16)
-    returned = lax.all_to_all(
-        total.reshape(experts, SLOTS, cols), "seq", split_axis=0, concat_axis=0, tiled=True
-    ).reshape(experts * SLOTS, cols)
+    slots = jnp.arange(SLOTS, dtype=jnp.int32)
+    place = (rank.T[:, None, :] == slots[None, :, None]) & picked.T[:, None, :]
+    pick = place.astype(BF16).reshape(8, experts // 8 * SLOTS, tok)
+    ranks = rank.reshape(tok, 8, 8).transpose(1, 0, 2)
+    taken = picked.reshape(tok, 8, 8).transpose(1, 0, 2)
+    gated = gate_of.reshape(tok, 8, 8).transpose(1, 0, 2)
+    weight = jnp.where((ranks[..., None] == slots) & taken[..., None], gated[..., None], 0.0)
+    weight = weight.reshape(8, tok, 8 * SLOTS)
     high = weight.astype(BF16)
     low = (weight - high.astype(F32)).astype(BF16)
-    moe = lax.dot_general(high, returned, (((0,), (0,)), ((), ())), preferred_element_type=F32)
-    moe = moe + lax.dot_general(low, returned, (((0,), (0,)), ((), ())), preferred_element_type=F32)
-    out = (residual.astype(F32) + moe).astype(BF16)
-    hidden_out = lax.all_gather(out, "head", axis=1, tiled=True)
+    hidden_out = run_experts(
+        mixed, w_expand, w_out, own_in, pick, high, low, moe_gain[None, :], w_gate, w_up, w_down, tok
+    )
 
     page_rows = latent.reshape(-1, PAGE * (LATENT + ROPE))
     slots_here = page_rows.shape[0] // n_head

time: 361 us -> 246 us (0.68)
  waiting for transfers between devices: 150 us -> 0 us
  Pallas kernels: 59.2 us -> 186 us
  blocking collectives: 59.1 us -> 8.5 us
  matrix products: 26.1 us -> 7.22 us
  between operations: 14.1 us -> 0.88 us
  starting transfers between devices: 12.9 us -> 0 us
  local copies, waits for them, and re-layouts: 23.1 us -> 28.3 us
    pallas_call x0 -> x1, Pallas kernels: none -> 127 us  [run_experts(): pl.pallas_call(experts_kernel, out_shape=jax.ShapeDtypeStruct((tok, D), B...]
    reduce_scatter x2 -> x0, waiting for transfers between devices: 81.6 us -> none  [the longest x1 48.7 us: local(): lax.psum_scatter(partial_out, 'head', scatter_dimension=1, tiled=True)]
    all_gather x1 -> x0, waiting for transfers between devices: 45.6 us -> none  [local(): rows = lax.all_gather(items, 'head', axis=0)]
    all_to_all x1 -> x0, blocking collectives: 41 us -> none  [local(): lax.all_to_all(outgoing.reshape(experts, SLOTS, cols), 'seq', split_axis=...]
    all_to_all x1 -> x0, waiting for transfers between devices: 23.1 us -> none  [local(): lax.all_to_all(total.reshape(experts, SLOTS, cols), 'seq', split_axis=0,...]
    dot_general x8 -> x4, matrix products: 19.3 us -> 5.76 us  [dot(): return jnp.dot(a, b, preferred_element_type=F32)]
    all_to_all x1 -> x0, starting transfers between devices: 12.6 us -> none  [local(): lax.all_to_all(total.reshape(experts, SLOTS, cols), 'seq', split_axis=0,...]
    all_gather x1 -> x0, blocking collectives: 9.65 us -> none  [local(): hidden_out = lax.all_gather(out, 'head', axis=1, tiled=True)]
  transfers between devices with their start and end apart: 4 -> 0, of which waited for: 4 -> 0; matrix products, arithmetic and copies ran while one was open for 2% -> 0% of each run, Pallas kernels for 0% -> 0%
where the time goes in v3:
time: 246 us; the launch traced here: 243 us
  Pallas kernels  186 us (76%)
  local copies, waits for them, and re-layouts  28.3 us (12%)
  other arithmetic  12.5 us (5%)
  blocking collectives  8.5 us (3%)
  matrix products  7.22 us (3%)
    pallas_call x1, Pallas kernels, run_experts(): pl.pallas_call(experts_kernel, out_shape=jax.ShapeDtypeStruct((tok, D), B...  127 us
    pallas_call x1, Pallas kernels, attend(): pl.pallas_call(functools.partial(attend_kernel, tok, heads), out_shape=ja...  59.2 us
    unnamed x18, local copies, waits for them, and re-layouts  11.9 us
    all_gather x1, blocking collectives, local(): latent_raw = lax.all_gather(latent_part, 'head', axis=1, tiled=True)  8.5 us
    dot_general x4, matrix products, dot(): return jnp.dot(a, b, preferred_element_type=F32)  5.76 us

profile of v3, /device:TPU:1, one launch (start us, length us, event | category | flops | bytes accessed | tf_op | source)
XLA Modules:
  0.0 243.5 jit_solution(17366049001733359591)
XLA Ops:
  0.7 1.4 fusion.1
  3.6 0.8 convolution_convert_fusion.1
  4.6 1.3 select_reduce_fusion
  5.9 1.6 convolution_convert_fusion
  7.6 8.5 %all_gather.3 = bf16[128,576]{0,1:T(8,128)(2,1)S(1)} all-gather(bf16[128,144]{0,1:T(8,128)(2,1)S(1)} %convolution_convert_fusion), channel_id=1, replica_groups=mesh['seq'=64,'head'=4] {'head'}, dimensions={1}, use_global_device_ids=true | all-gather | bytes 184320 | tf_op jit(solution)/shard_map/all_gather | solution.py:504
  17.1 0.8 concatenate.17
  17.9 1.4 constant_dynamic-slice_fusion.1.mine_ref
  19.3 0.7 pad_maximum_fusion
  20.0 1.1 reshape.159
  21.2 0.9 fusion.22
  22.7 1.6 constant_dynamic-slice_fusion.own_ref
  25.0 0.9 copy.91
  26.1 2.4 fusion.12
  29.3 0.8 copy.88
  30.0 0.9 fusion.15.qr_ref
  31.0 1.6 broadcast_in_dim.68
  32.6 2.0 copy.92
  34.6 0.8 eq.76
  35.4 1.8 fusion.6.pick_ref
  37.2 1.6 eq.82
  38.8 2.1 copy.90
  40.8 2.1 subtract_convert_fusion.low_ref
  42.9 2.1 fusion.17.high_ref
  45.0 2.3 copy.83
  47.3 1.5 fusion
  48.8 0.8 copy-done.2
  49.6 59.2 %shard_map.158.mixed_ref = bf16[512,512]{1,0:T(8,128)(2,1)S(1)} custom-call(bf16[32,640]{1,0:T(8,128)(2,1)S(1)} %copy-done.2, bf16[512,512]{1,0:T(8,128)(2,1)S(1)} %bitcast.43, bf16[528,128]{1,0:T(8,128)(2,1)S(1)} %fusion.15.qr_ref, f32[512,1]{1,0:T(8,128)S(1)} %copy.89.qseg_ref), custom_call_target="tpu_custom_call" | custom-call | tf_op jit(solution)/shard_map/pallas_call | solution.py:213
  108.8 0.8 copy-done.1
  109.6 2.6 %copy.93.wg_hbm = bf16[1,2048,352]{2,1,0:T(8,128)(2,1)} copy(bf16[1,2048,352]{1,2,0:T(8,128)(2,1)} %param.23) | data formatting | bytes 2883584 | tf_op args[8]
  112.2 2.6 %copy.94.wu_hbm = bf16[1,2048,352]{2,1,0:T(8,128)(2,1)} copy(bf16[1,2048,352]{1,2,0:T(8,128)(2,1)} %param.24) | data formatting | bytes 2883584 | tf_op args[9]
  114.7 126.9 %shard_map.159 = bf16[128,2048]{1,0:T(8,128)(2,1)} custom-call(bf16[512,512]{1,0:T(8,128)(2,1)} %copy-done.1, bf16[512,1024]{1,0:T(8,128)(2,1)} %expand_ref.1, bf16[512,2048]{1,0:T(8,128)(2,1)} %wout_ref.1, bf16[128,512]{1,0:T(8,128)(2,1)} %constant_dynamic-slice_fusion.own_ref, bf16[8,128,128]{2,1,0:T(8,128)(2,1)} %fusion.6.pick_ref, ...), custom_call_target="tpu_custom_call" | custom-call | tf_op jit(solution)/shard_map/pallas_call | solution.py:443
  241.6 1.9 copy.101
  (41 shorter events, 5.0 us)
Async XLA Ops:
  0.6 25.4 %copy-start = (bf16[2048,768]{1,0:T(8,128)(2,1)S(1)}, bf16[2048,768]{1,0:T(8,128)(2,1)}, u32[]{:S(2)}) copy-start(bf16[2048,768]{1,0:T(8,128)(2,1)} %param.17) | copy-start | bytes 9437188
  0.6 15.7 %copy-start.5 = (f32[512]{0:T(512)S(1)}, f32[512]{0:T(512)}, u32[]{:S(2)}) copy-start(f32[512]{0:T(512)} %param.19) | copy-start | bytes 6148
  16.1 9.9 %copy-start.4 = (f32[2048]{0:T(1024)S(1)}, f32[2048]{0:T(1024)}, u32[]{:S(2)}) copy-start(f32[2048]{0:T(1024)} %param.16) | copy-start | bytes 24580
  28.5 0.7 copy-start.3
  48.8 0.8 copy-start.2
  108.8 0.8 copy-start.1

commit v4 on v2

v4 whole, which is shorter than its diff:
```python
import jax
import jax.numpy as jnp
from jax import lax
from jax.experimental import pallas as pl
from jax.experimental.pallas import tpu as pltpu
from jax.sharding import PartitionSpec as P

D = 2048
NOPE = 128
ROPE = 64
VDIM = 128
LATENT = 512
TOPK = 6
TOK = 128
HEADS = 4
LONGEST = 6144
SLOTS = 16
KT = 512
PART = 32
WIDTH = 640

EPS = 1e-06
THETA = 50000.0
F32 = jnp.float32
BF16 = jnp.bfloat16


def rope_tables(positions, feat_width):
    half_width = feat_width // 2
    inv_freq = THETA ** (-jnp.arange(half_width, dtype=F32) * 2.0 / feat_width)
    angles = positions.astype(F32)[:, None] * inv_freq[None, :]
    return (jnp.cos(angles), jnp.sin(angles))


def dot(a, b):
    return jnp.dot(a, b, preferred_element_type=F32)


ORDER = ((0, 1), (7, 2), (6, 3), (5, 4))


def nt(a, b):
    return lax.dot_general(a, b, (((1,), (1,)), ((), ())), preferred_element_type=F32)


def place_of():
    seq, head = lax.axis_index("seq"), lax.axis_index("head")
    return seq // 8, (seq // 2) % 4, (seq % 2) * 2 + head // 2, head % 2


def device(z, x, y, core):
    return (z * 8 + x * 2 + y // 2, (y % 2) * 2 + core)


def remote(src, dst, send_sem, recv_sem, target):
    return pltpu.make_async_remote_copy(
        src_ref=src, dst_ref=dst, send_sem=send_sem, recv_sem=recv_sem,
        device_id=target, device_id_type=pl.DeviceIdType.MESH,
    )


def gather_keys(mine_ref, keys, work, own_sem, zs, zr, ps, pr, cs, cr):
    z, x, y, core = place_of()
    partner = device(z, x, y, 1 - core)
    up = lambda v: (v + 1) % 4
    down = lambda v: (v + 3) % 4
    z_peers = [device((z + d) % 8, x, y, core) for d in range(1, 8)]
    x_peers = (device(z, up(x), y, core), device(z, down(x), y, core))
    y_peers = (device(z, x, up(y), core), device(z, x, down(y), core))
    own = pltpu.make_async_copy(mine_ref, keys.at[z, x, y, core], own_sem)
    own.start()
    z_sends = []
    for d in (4, 3, 5, 2, 6, 1, 7):
        copy = remote(mine_ref, keys.at[z, x, y, core], zs.at[d - 1], zr.at[d - 1], z_peers[d - 1])
        copy.start()
        z_sends.append(copy)
    work()
    own.wait()
    for d in range(1, 8):
        there = keys.at[(z + 8 - d) % 8, x, y, core]
        remote(there, there, zs.at[d - 1], zr.at[d - 1], partner).wait_recv()

    def pieces(c, first):
        def one(along, lo, n, step):
            if along == "x":
                return keys.at[pl.ds(lo, n), (x + step) % 4, y, c]
            return keys.at[pl.ds(lo, n), x, (y + step) % 4, c]

        def two(along, lo, n, step):
            if along == "x":
                return keys.at[pl.ds(lo, n), (x + step) % 4, :, c]
            return keys.at[pl.ds(lo, n), :, (y + step) % 4, c]

        other = "y" if first == "x" else "x"
        out = [one(first, 0, 8, 0)]
        for form, along in ((one, first), (two, other)):
            out += [form(along, 0, 8, 3), form(along, 0, 8, 1), form(along, 0, 4, 2), form(along, 4, 4, 2)]
        return out, one, two

    def run(c, first):
        mine, one, two = pieces(c, first)
        theirs = pieces(1 - c, "y" if first == "x" else "x")[0]
        sends = []

        def share(i):
            copy = remote(mine[i], mine[i], cs.at[i], cr.at[i], partner)
            copy.start()
            sends.append(copy)

        share(0)
        other = "y" if first == "x" else "x"
        for ring, (form, along) in enumerate(((one, first), (two, other))):
            right, left = x_peers if along == "x" else y_peers
            base = 4 * ring

            def push(k, region, target):
                copy = remote(region, region, ps.at[base + k], pr.at[base + k], target)
                copy.start()
                sends.append(copy)

            def arrive(k):
                region = mine[1 + base + k]
                remote(region, region, ps.at[base + k], pr.at[base + k], partner).wait_recv()

            push(0, form(along, 0, 8, 0), right)
            push(1, form(along, 0, 8, 0), left)
            arrive(0)
            push(2, form(along, 0, 4, 3), right)
            share(1 + base)
            arrive(1)
            push(3, form(along, 4, 4, 1), left)
            share(2 + base)
            arrive(2)
            share(3 + base)
            arrive(3)
            share(4 + base)
        for i, region in enumerate(theirs):
            remote(region, region, cs.at[i], cr.at[i], partner).wait_recv()
        for copy in sends:
            copy.wait_send()

    @pl.when(core == 0)
    def _():
        run(0, "x")

    @pl.when(core == 1)
    def _():
        run(1, "y")

    for copy in z_sends:
        copy.wait_send()


def rotated(tile, cos, sin):
    lane = lax.broadcasted_iota(jnp.int32, tile.shape, 1)
    swapped = jnp.where(lane < ROPE // 2, pltpu.roll(tile, 96, 1), pltpu.roll(tile, 32, 1))
    return tile * cos + swapped * sin


def layer_kernel(
    hid_ref, again_ref, lgain_ref, mgain_ref, cos_ref, sin_ref, seg_ref, routes_ref, gates_ref, pages_ref,
    wl_hbm, wq_hbm, we_hbm, wo_hbm, wg_hbm, wu_hbm, wd_hbm, o_ref, cache_ref,
    wl, wq, we, wo, wg, wu, wd, normed, lpart, lall, tagged, keys, ql, qm, qbuf, m_ref, l_ref, acc_ref, mixed,
    pick, high, low, mix, apart, ain, res, outgoing, items, xin, pout, cin, ysend, yin, back, ret, acc, fin,
    w_sem, own_sem, ls, lr, zs_, zr_, ps, pr, cs, cr,
    rs, rr, a0s, a0r, as_, ar, fys, fyr, fps, fpr, fqs, fqr, xs, xr, ys, yr, b0s, b0r, bs, br, es, er,
):
    z, x, y, core = place_of()
    seq, head = lax.axis_index("seq"), lax.axis_index("head")
    yl, yh = head // 2, seq % 2
    partner = (seq, yl * 2 + 1 - core)
    across = (seq, (1 - yl) * 2 + core)
    q_partner = yl * 2 + 1 - core
    q_across = (1 - yl) * 2 + core
    q_far = (1 - yl) * 2 + 1 - core
    tok = TOK
    mesh_id = pl.DeviceIdType.MESH
    half_y = (y, 3 - y)
    half_h = (yh, 1 - yh)

    loads = [
        pltpu.make_async_copy(src, dst, w_sem.at[i])
        for i, (src, dst) in enumerate(
            (
                (wl_hbm, wl), (wq_hbm, wq), (we_hbm, we), (wo_hbm, wo),
                (wg_hbm.at[0], wg), (wu_hbm.at[0], wu), (wd_hbm.at[0], wd),
            )
        )
    ]
    for copy in loads:
        copy.start()

    barrier = pltpu.get_barrier_semaphore()
    column = z * 4 + x

    def greet(half, k):
        at = (column + k) % 32
        pl.semaphore_signal(
            barrier, inc=1, device_id=device(at // 4, at % 4, half_y[half], core), device_id_type=mesh_id
        )

    def greet_both(k, carry):
        greet(0, k)
        greet(1, k)
        return carry

    greet(1, 0)
    for d in range(1, 4):
        pl.semaphore_signal(barrier, inc=1, device_id=(seq, (head + d) % 4), device_id_type=mesh_id)
    lax.fori_loop(1, 32, greet_both, 0)

    sends = []

    def push(src, dst, send_sem, recv_sem, target):
        copy = remote(src, dst, send_sem, recv_sem, target)
        copy.start()
        sends.append(copy)

    def arrive(region, recv_sem):
        remote(region, region, own_sem.at[2], recv_sem, partner).wait_recv()

    v = hid_ref[...].astype(F32)
    inv = lax.rsqrt(jnp.sum(v * v, axis=1, keepdims=True) * (1.0 / D) + EPS)
    normed[...] = (v * inv * again_ref[...]).astype(BF16)
    lpart[...] = jnp.zeros_like(lpart)
    loads[0].wait()
    lpart[:, :144] = nt(normed[...], wl[...]).astype(BF16)
    pl.semaphore_wait(barrier, 66)

    for d in range(1, 4):
        push(lpart, lall.at[d - 1], ls.at[d - 1], lr.at[d - 1], (seq, (head + d) % 4))
    place_r = lax.broadcasted_iota(jnp.int32, (256, WIDTH), 0)
    place_c = lax.broadcasted_iota(jnp.int32, (256, WIDTH), 1)

    def spread(part, q):
        put = ((place_c == q * 144 + place_r) & (place_r < 144)).astype(F32).astype(BF16)
        return dot(part, put)

    raw = spread(lpart[...], head)
    for d in range(1, 4):
        arrive(lall.at[d - 1], lr.at[d - 1])
        raw = raw + spread(lall[d - 1], (head + 4 - d) % 4)
    comp = raw[:, :LATENT]
    inv = lax.rsqrt(jnp.sum(comp * comp, axis=1, keepdims=True) * (1.0 / LATENT) + EPS)
    tagged[:, :LATENT] = (comp * inv * lgain_ref[...]).astype(BF16)
    turned = rotated(raw[:, LATENT:], cos_ref[...], sin_ref[...])
    lane = lax.broadcasted_iota(jnp.int32, (tok, 128), 1)
    tagged[:, LATENT:] = jnp.where(lane == ROPE, seg_ref[...], turned).astype(BF16)

    scale = (NOPE + ROPE) ** (-0.5)

    def work():
        page = jnp.zeros((PART, WIDTH), BF16)
        for p in range(4):
            page = jnp.where(pages_ref[:, p : p + 1] == head, tagged[p * PART : (p + 1) * PART, :], page)
        cache_ref[...] = page[:, : LATENT + ROPE]
        loads[1].wait()
        qbuf[...] = dot(normed[...], wq[...])
        loads[2].wait()
        for k in range(HEADS // 2):
            t0 = qbuf[:, k * 384 : k * 384 + 128]
            t1 = qbuf[:, k * 384 + 128 : k * 384 + 256]
            t2 = pltpu.roll(qbuf[:, k * 384 + 256 : k * 384 + 384], 64, 1)
            nope = (t0, jnp.where(lane < 64, pltpu.roll(t1, 64, 1), t2))
            rope = (t1, t2)
            for i in range(2):
                h = 2 * k + i
                rows = slice(h * tok, (h + 1) * tok)
                key_w = we[:, h * (NOPE + VDIM) : h * (NOPE + VDIM) + NOPE]
                ql[rows, :] = (nt(nope[i].astype(BF16), key_w) * scale).astype(BF16)
                qm[rows, :] = (rotated(rope[i], cos_ref[...], sin_ref[...]) * scale).astype(BF16)
        qm[HEADS * tok :, :] = (lax.broadcasted_iota(jnp.int32, (16, 128), 1) == ROPE).astype(F32).astype(BF16)
        row = lax.broadcasted_iota(jnp.int32, (tok, 128), 0)
        below = (lane < row).astype(F32).astype(BF16)
        cell = lane // SLOTS
        slot = (lane % SLOTS).astype(F32)

        def table(ze, carry):
            expert = ze * 8 + (cell % 4) * 2 + cell // 4
            taken = jnp.zeros((tok, 128), F32)
            gate = jnp.zeros((tok, 128), F32)
            for j in range(TOPK):
                hit = routes_ref[:, j : j + 1] == expert
                taken = jnp.where(hit, 1.0, taken)
                gate = jnp.where(hit, gates_ref[:, j : j + 1], gate)
            rank = dot(below, taken.astype(BF16))
            put = (taken > 0.5) & (rank == slot)
            weight = jnp.where(put, gate, 0.0)
            top = weight.astype(BF16)
            high[ze] = top
            low[ze] = (weight - top.astype(F32)).astype(BF16)
            pick[ze] = put.astype(F32).T.astype(BF16)
            return carry

        lax.fori_loop(0, 8, table, 0)

    mine = tagged.at[pl.ds(pl.multiple_of(head * PART, PART), PART)]
    gather_keys(mine, keys, work, own_sem.at[3], zs_, zr_, ps, pr, cs, cr)

    rows = HEADS * tok
    m_ref[...] = jnp.full_like(m_ref, -1e30)
    l_ref[...] = jnp.zeros_like(l_ref)
    acc_ref[...] = jnp.zeros_like(acc_ref)
    qpos = seq * tok + lax.broadcasted_iota(jnp.int32, (rows, 1), 0) % tok
    qseg = jnp.concatenate([seg_ref[...]] * HEADS, axis=0)
    first = jnp.maximum(seq * tok - (LONGEST - 1), 0) // KT
    last = (seq * tok + tok - 1) // KT + 1

    def step(kt, carry):
        block = keys[kt // 2, pl.ds((kt % 2) * 2, 2)].reshape(KT, WIDTH)
        c = block[:, :LATENT]
        more = nt(qm[...], block[:, LATENT:])
        sc = nt(ql[...], c) + more[:rows]
        kseg = more[rows : rows + 1]
        kpos = kt * KT + lax.broadcasted_iota(jnp.int32, (1, KT), 1)
        ok = (qseg == kseg) & (kpos <= qpos)
        sc = jnp.where(ok, sc, -1e30)
        m_old = m_ref[...]
        m_new = jnp.maximum(m_old, jnp.max(sc, axis=1, keepdims=True))
        p = jnp.where(ok, jnp.exp(sc - m_new), 0.0)
        fade = jnp.exp(m_old - m_new)
        l_ref[...] = l_ref[...] * fade + jnp.sum(p, axis=1, keepdims=True)
        acc_ref[...] = acc_ref[...] * fade + dot(p.astype(BF16), c)
        m_ref[...] = m_new
        return carry

    lax.fori_loop(first, last, step, 0)
    mixed[...] = (acc_ref[...] / l_ref[...]).astype(BF16)

    for h in range(HEADS):
        value = we[:, h * (NOPE + VDIM) + NOPE : (h + 1) * (NOPE + VDIM)]
        mix[:, h * VDIM : (h + 1) * VDIM] = dot(mixed[h * tok : (h + 1) * tok, :], value).astype(BF16)
    loads[3].wait()
    for q in range(4):
        apart[q] = dot(mix[...], wo[:, q * 512 : (q + 1) * 512]).astype(BF16)
    for d in range(1, 4):
        q = (head + d) % 4
        push(apart.at[q], ain.at[d - 1], rs.at[d - 1], rr.at[d - 1], (seq, q))
    total = apart[head].astype(F32)
    for d in range(1, 4):
        arrive(ain.at[d - 1], rr.at[d - 1])
        total = total + ain[d - 1].astype(F32)
    own = hid_ref[:, pl.ds(pl.multiple_of(head * 512, 512), 512)].astype(F32)
    res[...] = (own + total).astype(BF16)

    locals_ = []

    def send_slab(src, dst, slab, j, send0, recv0, send_sem, recv_sem, local_sem):
        for half in range(2):
            if half == 0 and j == 0:
                copy = pltpu.make_async_copy(src.at[slab, yh, x], dst.at[z, yh, x], local_sem)
                copy.start()
                locals_.append(copy)
                for k in range(1, 4):
                    xt = (x + k) % 4
                    push(
                        src.at[slab, yh, xt], dst.at[z, yh, x], send0.at[k - 1], recv0.at[k - 1],
                        device(slab, xt, y, core),
                    )
            else:

                def send(xt, carry, half=half):
                    remote(
                        src.at[slab, half_h[half], xt], dst.at[z, yh, x], send_sem.at[half, j], recv_sem.at[half, j],
                        device(slab, xt, half_y[half], core),
                    ).start()
                    return carry

                lax.fori_loop(0, 4, send, 0)

    def slab_sent(src, slab, j, send_sem):
        for half in range(2):
            if half or j:
                part = src.at[slab, half_h[half]]
                remote(part, part, send_sem.at[half, j], own_sem.at[2], partner).wait_send()

    def slab_arrived(parts, j, recv0, recv_sem, local):
        for half in range(2):
            if half == 0 and j == 0:
                locals_[local].wait()
                for k in range(1, 4):
                    arrive(parts[0].at[(x + 4 - k) % 4], recv0.at[k - 1])
            else:
                arrive(parts[half], recv_sem.at[half, j])

    for pair in ORDER:
        for j in pair:
            zt = (z + j) % 8
            outgoing[zt] = dot(pick[zt], res[...]).astype(BF16).reshape(2, 4, SLOTS, 512)
            send_slab(outgoing, items.at[head], zt, j, a0s, a0r, as_, ar, own_sem.at[0])

    def stage_a(g):
        for j in ORDER[g]:
            zs = (z + 8 - j) % 8
            parts = (items.at[head, zs, yh], items.at[q_across, zs, 1 - yh])
            slab_arrived(parts, j, a0r, ar, 0)
            for half in range(2):
                push(parts[half], parts[half], fys.at[half, j], fyr.at[half, j], across)
                push(parts[half], parts[half], fps.at[half, j], fpr.at[half, j], partner)

    def stage_b(g):
        for j in ORDER[g]:
            zs = (z + 8 - j) % 8
            for half, part in enumerate((items.at[q_across, zs, yh], items.at[head, zs, 1 - yh])):
                arrive(part, fyr.at[half, j])
                push(part, part, fqs.at[half, j], fqr.at[half, j], partner)

    def stage_c(g):
        if g == 0:
            for copy in loads[4:]:
                copy.wait()
        for t, j in enumerate(ORDER[g]):
            zs = (z + 8 - j) % 8
            arrive(items.at[q_partner, zs, yh], fpr.at[0, j])
            arrive(items.at[q_far, zs, 1 - yh], fpr.at[1, j])
            arrive(items.at[q_far, zs, yh], fqr.at[0, j])
            arrive(items.at[q_partner, zs, 1 - yh], fqr.at[1, j])
            mean_sq = jnp.zeros((tok, 1), F32)
            for q in range(4):
                v = items[q, zs].reshape(tok, 512).astype(F32)
                mean_sq = mean_sq + jnp.sum(v * v, axis=1, keepdims=True)
            inv = lax.rsqrt(mean_sq * (1.0 / D) + EPS)
            for q in range(4):
                v = items[q, zs].reshape(tok, 512).astype(F32)
                cols = slice(q * 512, (q + 1) * 512)
                xin[t * tok : (t + 1) * tok, cols] = (v * inv * mgain_ref[:, cols]).astype(BF16)
        gate = nt(xin[...], wg[...])
        up = nt(xin[...], wu[...])
        hidden = (gate / (1.0 + jnp.exp(-gate)) * up).astype(BF16)
        for q in range(4):
            part = dot(hidden, wd[:, q * 512 : (q + 1) * 512]).astype(BF16)
            for t, j in enumerate(ORDER[g]):
                pout[q, (z + 8 - j) % 8] = part[t * tok : (t + 1) * tok].reshape(2, 4, SLOTS, 512)
        for j in ORDER[g]:
            zs = (z + 8 - j) % 8
            for side in range(2):
                push(
                    pout.at[side * 2 + 1 - core, zs], cin.at[side, zs], xs.at[side, j], xr.at[side, j], partner
                )

    def chip_sum(side, zs, h):
        return pout[side * 2 + core, zs, h].astype(F32) + cin[side, zs, h].astype(F32)

    def stage_d(g):
        for j in ORDER[g]:
            zs = (z + 8 - j) % 8
            for side in range(2):
                arrive(cin.at[side, zs], xr.at[side, j])
            ysend[zs, yh] = chip_sum(1 - yl, zs, yh).astype(BF16)
            ysend[zs, 1 - yh] = chip_sum(yl, zs, 1 - yh).astype(BF16)
            push(ysend.at[zs], yin.at[zs], ys.at[j], yr.at[j], across)

    def stage_e(g):
        for j in ORDER[g]:
            zs = (z + 8 - j) % 8
            arrive(yin.at[zs], yr.at[j])
            back[zs, yh] = (chip_sum(yl, zs, yh) + yin[zs, yh].astype(F32)).astype(BF16)
            back[zs, 1 - yh] = (chip_sum(1 - yl, zs, 1 - yh) + yin[zs, 1 - yh].astype(F32)).astype(BF16)
            send_slab(back, ret, zs, j, b0s, b0r, bs, br, own_sem.at[1])

    a, b, c, d, e = stage_a, stage_b, stage_c, stage_d, stage_e
    for stage, g in (
        (a, 0), (b, 0), (a, 1), (c, 0), (b, 1), (d, 0), (a, 2), (c, 1), (e, 0), (b, 2),
        (d, 1), (a, 3), (c, 2), (e, 1), (b, 3), (d, 2), (c, 3), (e, 2), (d, 3), (e, 3),
    ):
        stage(g)

    acc[...] = res[...].astype(F32)
    for pair in ORDER:
        for j in pair:
            ze = (z + j) % 8
            slab_arrived((ret.at[ze, yh], ret.at[ze, 1 - yh]), j, b0r, br, 1)
            got = ret[ze].reshape(tok, 512)
            acc[...] += dot(high[ze], got) + dot(low[ze], got)
    fin[head] = acc[...].astype(BF16)
    push(fin.at[head], fin.at[head], es.at[0], er.at[0], across)
    push(fin.at[head], fin.at[head], es.at[1], er.at[1], partner)
    arrive(fin.at[q_across], er.at[0])
    push(fin.at[q_across], fin.at[q_across], es.at[2], er.at[2], partner)
    arrive(fin.at[q_partner], er.at[1])
    arrive(fin.at[q_far], er.at[2])
    for q in range(4):
        o_ref[:, q * 512 : (q + 1) * 512] = fin[q]
    for copy in sends:
        copy.wait_send()
    for j in range(8):
        slab_sent(outgoing, (z + j) % 8, j, as_)
        slab_sent(back, (z + 8 - j) % 8, j, bs)


def local(
    hidden_in,
    attn_gain,
    w_query,
    w_latent,
    latent_gain,
    w_expand,
    w_out,
    moe_gain,
    w_gate,
    w_up,
    w_down,
    routes,
    gates,
    segment,
    page_table,
):
    positions = lax.axis_index("seq") * TOK + jnp.arange(TOK, dtype=jnp.int32)
    cosine, sine = rope_tables(positions, ROPE)
    rest = jnp.zeros((TOK, 128 - ROPE), F32)
    cos = jnp.concatenate([cosine, cosine, rest], axis=1)
    sin = jnp.concatenate([-sine, sine, rest], axis=1)
    ff = w_gate.shape[2]
    dma = pltpu.SemaphoreType.DMA
    vmem, hbm = pl.BlockSpec(memory_space=pltpu.VMEM), pl.BlockSpec(memory_space=pl.ANY)
    chunks = (8, 2, 4, SLOTS, 512)
    quarter = (TOK, 512)
    rows = HEADS * TOK
    tables = (8, 128, 128)

    def space(*shape):
        return pltpu.VMEM(shape, BF16)

    def two(*shape):
        return [dma(shape), dma(shape)]

    hidden_out, page = pl.pallas_call(
        layer_kernel,
        out_shape=(
            jax.ShapeDtypeStruct((TOK, D), BF16),
            jax.ShapeDtypeStruct((PART, LATENT + ROPE), BF16),
        ),
        in_specs=[vmem] * 10 + [hbm] * 7,
        out_specs=(vmem, vmem),
        scratch_shapes=[
            space(144, D), space(D, 768), space(LATENT, 1024), space(512, D), space(ff, D), space(ff, D),
            space(ff, D), space(TOK, D), space(TOK, 256), space(3, TOK, 256), space(TOK, WIDTH),
            space(8, 4, 4, 2, PART, WIDTH), space(rows, LATENT), space(rows + 16, 128),
            pltpu.VMEM((TOK, 768), F32), pltpu.VMEM((rows, 1), F32), pltpu.VMEM((rows, 1), F32),
            pltpu.VMEM((rows, LATENT), F32), space(rows, LATENT),
            space(*tables), space(*tables), space(*tables), space(*quarter), space(4, *quarter),
            space(3, *quarter), space(*quarter), space(*chunks), space(4, *chunks), space(2 * TOK, D),
            space(4, *chunks), space(2, *chunks), space(*chunks), space(*chunks), space(*chunks), space(*chunks),
            pltpu.VMEM(quarter, F32), space(4, *quarter),
            dma((7,)), dma((4,)), *two(3), *two(7), *two(8), *two(9),
            *two(3), *two(3), *two(2, 8), *two(2, 8), *two(2, 8), *two(2, 8), *two(2, 8), *two(8),
            *two(3), *two(2, 8), *two(3),
        ],
        compiler_params=pltpu.CompilerParams(
            collective_id=0, has_side_effects=True, vmem_limit_bytes=60 << 20
        ),
    )(
        hidden_in,
        attn_gain[None, :],
        latent_gain[None, :],
        moe_gain[None, :],
        cos,
        sin,
        segment[:, None].astype(F32),
        routes,
        gates,
        page_table,
        w_latent.T,
        w_query,
        w_expand,
        w_out,
        w_gate.transpose(0, 2, 1),
        w_up.transpose(0, 2, 1),
        w_down,
    )
    return (hidden_out, page.reshape(1, PART * (LATENT + ROPE)))


def solution(mesh):
    return jax.shard_map(
        local,
        mesh=mesh,
        in_specs=(
            P("seq", None),
            P(),
            P(None, "head"),
            P(None, "head"),
            P(),
            P(None, "head"),
            P("head", None),
            P(),
            P("seq", None, "head"),
            P("seq", None, "head"),
            P("seq", "head", None),
            P("seq", None),
            P("seq", None),
            P("seq"),
            P("seq", None),
        ),
        out_specs=(P("seq", None), P(("seq", "head"), None)),
        check_vma=False,
    )
```

time: 361 us -> 190 us (0.53)
  the two profiles are of different devices: /device:TPU:1 before, /device:TPU:73 now
where the time goes in v4:
time: 190 us
  Pallas kernels  180 us (95%)
  local copies, waits for them, and re-layouts  7.05 us (4%)
    pallas_call x1, Pallas kernels, local(): pl.pallas_call(layer_kernel, out_shape=(jax.ShapeDtypeStruct((TOK, D), BF...  180 us
    unnamed x3, local copies, waits for them, and re-layouts  4.71 us

profile of v4, /device:TPU:73, one launch (start us, length us, event | category | flops | bytes accessed | tf_op | source)
XLA Modules:
  0.0 189.9 jit_solution(648838734505067087)
XLA Ops:
  0.6 0.7 convert_bitcast_fusion
  1.3 0.1 pad.5.clone
  1.4 0.7 copy.21.seg_ref
  2.1 1.4 copy.22.routes_ref
  3.6 1.4 copy.23.gates_ref
  5.0 0.3 fusion
  5.3 0.8 maximum_maximum_fusion.1
  6.0 180.4 %shard_map.158 = (bf16[128,2048]{1,0:T(8,128)(2,1)}, bf16[32,576]{1,0:T(8,128)(2,1)}) custom-call(bf16[128,2048]{1,0:T(8,128)(2,1)} %hid_ref.1, f32[1,2048]{1,0:T(1,128)} %bitcast.11, f32[1,512]{1,0:T(1,128)} %bitcast.13, f32[1,2048]{1,0:T(1,128)} %bitcast.12, f32[128,128]{1,0:T(8,128)} %get-tuple-element.10.cos_ref, f32[128,128]{1,0:T(8,128)} %get-tuple-element.9.sin_ref, ...), custom_call_target="tpu_custom_call" | custom-call | tf_op jit(solution)/shard_map/pallas_call | solution.py:527
  186.4 1.5 reshape.19
  188.0 1.9 copy.25
  (3 shorter events, 0.0 us)

commit v5 on v4

--- a/solution.py
+++ b/solution.py
@@ -13,9 +13,7 @@
 TOPK = 6
 TOK = 128
 HEADS = 4
-LONGEST = 6144
 SLOTS = 16
-KT = 512
 PART = 32
 WIDTH = 640
 
@@ -59,96 +57,120 @@
     )
 
 
-def gather_keys(mine_ref, keys, work, own_sem, zs, zr, ps, pr, cs, cr):
-    z, x, y, core = place_of()
-    partner = device(z, x, y, 1 - core)
-    up = lambda v: (v + 1) % 4
-    down = lambda v: (v + 3) % 4
-    z_peers = [device((z + d) % 8, x, y, core) for d in range(1, 8)]
-    x_peers = (device(z, up(x), y, core), device(z, down(x), y, core))
-    y_peers = (device(z, x, up(y), core), device(z, x, down(y), core))
-    own = pltpu.make_async_copy(mine_ref, keys.at[z, x, y, core], own_sem)
-    own.start()
-    z_sends = []
-    for d in (4, 3, 5, 2, 6, 1, 7):
-        copy = remote(mine_ref, keys.at[z, x, y, core], zs.at[d - 1], zr.at[d - 1], z_peers[d - 1])
-        copy.start()
-        z_sends.append(copy)
-    work()
-    own.wait()
-    for d in range(1, 8):
-        there = keys.at[(z + 8 - d) % 8, x, y, core]
-        remote(there, there, zs.at[d - 1], zr.at[d - 1], partner).wait_recv()
-
-    def pieces(c, first):
-        def one(along, lo, n, step):
-            if along == "x":
-                return keys.at[pl.ds(lo, n), (x + step) % 4, y, c]
-            return keys.at[pl.ds(lo, n), x, (y + step) % 4, c]
-
-        def two(along, lo, n, step):
-            if along == "x":
-                return keys.at[pl.ds(lo, n), (x + step) % 4, :, c]
-            return keys.at[pl.ds(lo, n), :, (y + step) % 4, c]
-
-        other = "y" if first == "x" else "x"
-        out = [one(first, 0, 8, 0)]
-        for form, along in ((one, first), (two, other)):
-            out += [form(along, 0, 8, 3), form(along, 0, 8, 1), form(along, 0, 4, 2), form(along, 4, 4, 2)]
-        return out, one, two
-
-    def run(c, first):
-        mine, one, two = pieces(c, first)
-        theirs = pieces(1 - c, "y" if first == "x" else "x")[0]
-        sends = []
-
-        def share(i):
-            copy = remote(mine[i], mine[i], cs.at[i], cr.at[i], partner)
+NEAR = 7
+HALVES = ((0, 4), (4, 3))
+
+
+class KeyGather:
+    def __init__(self, keys, own_sem, zs, zr, ps, pr, cs, cr):
+        self.keys, self.own_sem = keys, own_sem
+        self.zs, self.zr, self.ps, self.pr, self.cs, self.cr = zs, zr, ps, pr, cs, cr
+        self.z, self.x, self.y, self.core = place_of()
+        self.partner = device(self.z, self.x, self.y, 1 - self.core)
+
+    def both(self, act):
+        @pl.when(self.core == 0)
+        def _():
+            act(0)
+
+        @pl.when(self.core == 1)
+        def _():
+            act(1)
+
+    def region(self, c, ring, lo, n, step):
+        along_x = (c == 0) == (ring == 0)
+        planes = pl.ds(lo, n)
+        if along_x:
+            at = (self.x + step) % 4
+            return self.keys.at[planes, at, self.y, c] if ring == 0 else self.keys.at[planes, at, :, c]
+        at = (self.y + step) % 4
+        return self.keys.at[planes, self.x, at, c] if ring == 0 else self.keys.at[planes, :, at, c]
+
+    def piece(self, c, i):
+        if i == 0:
+            return self.region(c, 0, 0, NEAR, 0)
+        lo, n, step = ((0, NEAR, 3), (0, NEAR, 1), (*HALVES[0], 2), (*HALVES[1], 2))[(i - 1) % 4]
+        return self.region(c, (i - 1) // 4, lo, n, step)
+
+    def share(self, c, i):
+        part = self.piece(c, i)
+        return remote(part, part, self.cs.at[i], self.cr.at[i], self.partner)
+
+    def shared(self, c, i):
+        part = self.piece(1 - c, i)
+        remote(part, part, self.cs.at[i], self.cr.at[i], self.partner).wait_recv()
+
+    def push(self, c, ring, k):
+        along_x = (c == 0) == (ring == 0)
+        x, y, z = self.x, self.y, self.z
+        turn = 1 if k in (0, 2) else 3
+        to = device(z, (x + turn) % 4, y, self.core) if along_x else device(z, x, (y + turn) % 4, self.core)
+        lo, n, step = ((0, NEAR, 0), (0, NEAR, 0), (*HALVES[0], 3), (*HALVES[1], 1))[k]
+        part = self.region(c, ring, lo, n, step)
+        return remote(part, part, self.ps.at[4 * ring + k], self.pr.at[4 * ring + k], to)
+
+    def arrive(self, c, ring, k):
+        part = self.piece(c, 1 + 4 * ring + k)
+        remote(part, part, self.ps.at[4 * ring + k], self.pr.at[4 * ring + k], self.partner).wait_recv()
+
+    def along_z(self, mine_ref):
+        slot = lambda r: self.keys.at[r, self.x, self.y, self.core]
+        own = pltpu.make_async_copy(mine_ref, slot(NEAR - 1), self.own_sem)
+        own.start()
+        copies = []
+        for d in (4, 3, 5, 2, 6, 1):
+            to = device((self.z + d) % 8, self.x, self.y, self.core)
+            copy = remote(mine_ref, slot(NEAR - 1 - d), self.zs.at[d - 1], self.zr.at[d - 1], to)
             copy.start()
-            sends.append(copy)
-
-        share(0)
-        other = "y" if first == "x" else "x"
-        for ring, (form, along) in enumerate(((one, first), (two, other))):
-            right, left = x_peers if along == "x" else y_peers
-            base = 4 * ring
-
-            def push(k, region, target):
-                copy = remote(region, region, ps.at[base + k], pr.at[base + k], target)
-                copy.start()
-                sends.append(copy)
-
-            def arrive(k):
-                region = mine[1 + base + k]
-                remote(region, region, ps.at[base + k], pr.at[base + k], partner).wait_recv()
-
-            push(0, form(along, 0, 8, 0), right)
-            push(1, form(along, 0, 8, 0), left)
-            arrive(0)
-            push(2, form(along, 0, 4, 3), right)
-            share(1 + base)
-            arrive(1)
-            push(3, form(along, 4, 4, 1), left)
-            share(2 + base)
-            arrive(2)
-            share(3 + base)
-            arrive(3)
-            share(4 + base)
-        for i, region in enumerate(theirs):
-            remote(region, region, cs.at[i], cr.at[i], partner).wait_recv()
-        for copy in sends:
+            copies.append(copy)
+        yield
+        own.wait()
+        for copy in copies:
             copy.wait_send()
-
-    @pl.when(core == 0)
-    def _():
-        run(0, "x")
-
-    @pl.when(core == 1)
-    def _():
-        run(1, "y")
-
-    for copy in z_sends:
-        copy.wait_send()
+        for d in range(1, NEAR):
+            there = slot(NEAR - 1 - d)
+            remote(there, there, self.zs.at[d - 1], self.zr.at[d - 1], self.partner).wait_recv()
+        yield
+
+    def first_rings(self, c):
+        self.share(c, 0).start()
+        self.push(c, 0, 0).start()
+        self.push(c, 0, 1).start()
+        for k in range(4):
+            self.arrive(c, 0, k)
+            if k < 2:
+                self.push(c, 0, 2 + k).start()
+            if k == 3:
+                self.push(c, 1, 0).start()
+                self.push(c, 1, 1).start()
+        for k in range(4):
+            self.share(c, 1 + k).start()
+        for i in range(5):
+            self.shared(c, i)
+
+    def next_lines(self, c):
+        for k in range(2):
+            self.arrive(c, 1, k)
+            self.push(c, 1, 2 + k).start()
+            self.share(c, 5 + k).start()
+        for i in (5, 6):
+            self.shared(c, i)
+
+    def last_line(self, c):
+        for k in (2, 3):
+            self.arrive(c, 1, k)
+            self.share(c, 5 + k).start()
+
+    def last_shared(self, c):
+        for i in (7, 8):
+            self.shared(c, i)
+
+    def drain(self, c):
+        for i in range(9):
+            self.share(c, i).wait_send()
+        for ring in range(2):
+            for k in range(4):
+                self.push(c, ring, k).wait_send()
 
 
 def rotated(tile, cos, sin):
@@ -161,7 +183,7 @@
     hid_ref, again_ref, lgain_ref, mgain_ref, cos_ref, sin_ref, seg_ref, routes_ref, gates_ref, pages_ref,
     wl_hbm, wq_hbm, we_hbm, wo_hbm, wg_hbm, wu_hbm, wd_hbm, o_ref, cache_ref,
     wl, wq, we, wo, wg, wu, wd, normed, lpart, lall, tagged, keys, ql, qm, qbuf, m_ref, l_ref, acc_ref, mixed,
-    pick, high, low, mix, apart, ain, res, outgoing, items, xin, pout, cin, ysend, yin, back, ret, acc, fin,
+    turn, pick, high, low, mix, apart, ain, res, outgoing, items, xin, pout, cin, ysend, yin, back, ret, acc, fin,
     w_sem, own_sem, ls, lr, zs_, zr_, ps, pr, cs, cr,
     rs, rr, a0s, a0r, as_, ar, fys, fyr, fps, fpr, fqs, fqr, xs, xr, ys, yr, b0s, b0r, bs, br, es, er,
 ):
@@ -223,6 +245,12 @@
     inv = lax.rsqrt(jnp.sum(v * v, axis=1, keepdims=True) * (1.0 / D) + EPS)
     normed[...] = (v * inv * again_ref[...]).astype(BF16)
     lpart[...] = jnp.zeros_like(lpart)
+    turn[...] = jnp.zeros_like(turn)
+    turn[0:TOPK, :] = routes_ref[...].astype(F32)
+    turn[8 : 8 + TOPK, :] = gates_ref[...]
+    turn[16:17, :] = seg_ref[...].astype(F32)
+    turn[...] = turn[...].T
+    seg_col = turn[:, 16:17]
     loads[0].wait()
     lpart[:, :144] = nt(normed[...], wl[...]).astype(BF16)
     pl.semaphore_wait(barrier, 66)
@@ -245,7 +273,7 @@
     tagged[:, :LATENT] = (comp * inv * lgain_ref[...]).astype(BF16)
     turned = rotated(raw[:, LATENT:], cos_ref[...], sin_ref[...])
     lane = lax.broadcasted_iota(jnp.int32, (tok, 128), 1)
-    tagged[:, LATENT:] = jnp.where(lane == ROPE, seg_ref[...], turned).astype(BF16)
+    tagged[:, LATENT:] = jnp.where(lane == ROPE, seg_col, turned).astype(BF16)
 
     scale = (NOPE + ROPE) ** (-0.5)
 
@@ -276,13 +304,13 @@
         slot = (lane % SLOTS).astype(F32)
 
         def table(ze, carry):
-            expert = ze * 8 + (cell % 4) * 2 + cell // 4
+            expert = (ze * 8 + (cell % 4) * 2 + cell // 4).astype(F32)
             taken = jnp.zeros((tok, 128), F32)
             gate = jnp.zeros((tok, 128), F32)
             for j in range(TOPK):
-                hit = routes_ref[:, j : j + 1] == expert
+                hit = turn[:, j : j + 1] == expert
                 taken = jnp.where(hit, 1.0, taken)
-                gate = jnp.where(hit, gates_ref[:, j : j + 1], gate)
+                gate = jnp.where(hit, turn[:, 8 + j : 9 + j], gate)
             rank = dot(below, taken.astype(BF16))
             put = (taken > 0.5) & (rank == slot)
             weight = jnp.where(put, gate, 0.0)
@@ -295,36 +323,71 @@
         lax.fori_loop(0, 8, table, 0)
 
     mine = tagged.at[pl.ds(pl.multiple_of(head * PART, PART), PART)]
-    gather_keys(mine, keys, work, own_sem.at[3], zs_, zr_, ps, pr, cs, cr)
-
+    gather = KeyGather(keys, own_sem.at[3], zs_, zr_, ps, pr, cs, cr)
+    first = gather.along_z(mine)
+    next(first)
+    work()
     rows = HEADS * tok
     m_ref[...] = jnp.full_like(m_ref, -1e30)
     l_ref[...] = jnp.zeros_like(l_ref)
     acc_ref[...] = jnp.zeros_like(acc_ref)
     qpos = seq * tok + lax.broadcasted_iota(jnp.int32, (rows, 1), 0) % tok
-    qseg = jnp.concatenate([seg_ref[...]] * HEADS, axis=0)
-    first = jnp.maximum(seq * tok - (LONGEST - 1), 0) // KT
-    last = (seq * tok + tok - 1) // KT + 1
-
-    def step(kt, carry):
-        block = keys[kt // 2, pl.ds((kt % 2) * 2, 2)].reshape(KT, WIDTH)
-        c = block[:, :LATENT]
-        more = nt(qm[...], block[:, LATENT:])
-        sc = nt(ql[...], c) + more[:rows]
-        kseg = more[rows : rows + 1]
-        kpos = kt * KT + lax.broadcasted_iota(jnp.int32, (1, KT), 1)
-        ok = (qseg == kseg) & (kpos <= qpos)
-        sc = jnp.where(ok, sc, -1e30)
-        m_old = m_ref[...]
-        m_new = jnp.maximum(m_old, jnp.max(sc, axis=1, keepdims=True))
-        p = jnp.where(ok, jnp.exp(sc - m_new), 0.0)
-        fade = jnp.exp(m_old - m_new)
-        l_ref[...] = l_ref[...] * fade + jnp.sum(p, axis=1, keepdims=True)
-        acc_ref[...] = acc_ref[...] * fade + dot(p.astype(BF16), c)
-        m_ref[...] = m_new
+    qseg = jnp.concatenate([seg_col] * HEADS, axis=0)
+
+    def attend(color, line):
+        for lo, n in HALVES:
+            parts = []
+            for k in range(4):
+                xx = jnp.where(color == 0, k, line)
+                yy = jnp.where(color == 0, line, k)
+                parts.append(keys[pl.ds(lo, n), xx, yy, color].reshape(n * PART, WIDTH))
+            block = jnp.concatenate(parts, axis=0)
+            at = lax.broadcasted_iota(jnp.int32, (1, n * 128), 1)
+            turn_k = at // (n * PART)
+            plane = (z + 2 + lo + (at // PART) % n) % 8
+            kpos = plane * 1024 + color * PART + at % PART
+            kpos = kpos + jnp.where(color == 0, turn_k * 256 + line * 64, line * 256 + turn_k * 64)
+            c = block[:, :LATENT]
+            more = nt(qm[...], block[:, LATENT:])
+            sc = nt(ql[...], c) + more[:rows]
+            kseg = more[rows : rows + 1]
+            ok = (qseg == kseg) & (kpos <= qpos)
+            sc = jnp.where(ok, sc, -1e30)
+            m_old = m_ref[...]
+            m_new = jnp.maximum(m_old, jnp.max(sc, axis=1, keepdims=True))
+            p = jnp.where(ok, jnp.exp(sc - m_new), 0.0)
+            fade = jnp.exp(m_old - m_new)
+            l_ref[...] = l_ref[...] * fade + jnp.sum(p, axis=1, keepdims=True)
+            acc_ref[...] = acc_ref[...] * fade + dot(p.astype(BF16), c)
+            m_ref[...] = m_new
+
+    def attend_lines(steps):
+        def one(t, carry):
+            color = t % 2
+            step = steps[0] if len(steps) == 1 else 1 + 2 * (t // 2)
+            attend(color, (jnp.where(color == 0, y, x) + step) % 4)
+            return carry
+
+        lax.fori_loop(0, 2 * len(steps), one, 0)
+
+    next(first)
+    gather.both(gather.first_rings)
+    attend_lines((0,))
+    gather.both(gather.next_lines)
+    attend_lines((1, 3))
+    gather.both(gather.last_line)
+
+    def last(t, carry):
+        @pl.when(t == 1)
+        def _():
+            gather.both(gather.last_shared)
+
+        color = (core + t) % 2
+        attend(color, (jnp.where(color == 0, y, x) + 2) % 4)
         return carry
 
-    lax.fori_loop(first, last, step, 0)
+    lax.fori_loop(0, 2, last, 0)
+    gather.both(gather.drain)
     mixed[...] = (acc_ref[...] / l_ref[...]).astype(BF16)
 
     for h in range(HEADS):
@@ -473,12 +536,16 @@
             got = ret[ze].reshape(tok, 512)
             acc[...] += dot(high[ze], got) + dot(low[ze], got)
     fin[head] = acc[...].astype(BF16)
-    push(fin.at[head], fin.at[head], es.at[0], er.at[0], across)
-    push(fin.at[head], fin.at[head], es.at[1], er.at[1], partner)
-    arrive(fin.at[q_across], er.at[0])
-    push(fin.at[q_across], fin.at[q_across], es.at[2], er.at[2], partner)
-    arrive(fin.at[q_partner], er.at[1])
-    arrive(fin.at[q_far], er.at[2])
+    parts = (pl.ds(0, tok // 2), pl.ds(tok // 2, tok // 2))
+    for i, at in enumerate(parts):
+        push(fin.at[head, at], fin.at[head, at], es.at[i], er.at[i], across)
+    push(fin.at[head], fin.at[head], es.at[4], er.at[4], partner)
+    for i, at in enumerate(parts):
+        arrive(fin.at[q_across, at], er.at[i])
+        push(fin.at[q_across, at], fin.at[q_across, at], es.at[2 + i], er.at[2 + i], partner)
+    arrive(fin.at[q_partner], er.at[4])
+    for i, at in enumerate(parts):
+        arrive(fin.at[q_far, at], er.at[2 + i])
     for q in range(4):
         o_ref[:, q * 512 : (q + 1) * 512] = fin[q]
     for copy in sends:
@@ -535,16 +602,17 @@
         scratch_shapes=[
             space(144, D), space(D, 768), space(LATENT, 1024), space(512, D), space(ff, D), space(ff, D),
             space(ff, D), space(TOK, D), space(TOK, 256), space(3, TOK, 256), space(TOK, WIDTH),
-            space(8, 4, 4, 2, PART, WIDTH), space(rows, LATENT), space(rows + 16, 128),
+            space(NEAR, 4, 4, 2, PART, WIDTH), space(rows, LATENT), space(rows + 16, 128),
             pltpu.VMEM((TOK, 768), F32), pltpu.VMEM((rows, 1), F32), pltpu.VMEM((rows, 1), F32),
             pltpu.VMEM((rows, LATENT), F32), space(rows, LATENT),
-            space(*tables), space(*tables), space(*tables), space(*quarter), space(4, *quarter),
+            pltpu.VMEM((TOK, 128), F32), space(*tables), space(*tables), space(*tables), space(*quarter),
+            space(4, *quarter),
             space(3, *quarter), space(*quarter), space(*chunks), space(4, *chunks), space(2 * TOK, D),
             space(4, *chunks), space(2, *chunks), space(*chunks), space(*chunks), space(*chunks), space(*chunks),
             pltpu.VMEM(quarter, F32), space(4, *quarter),
-            dma((7,)), dma((4,)), *two(3), *two(7), *two(8), *two(9),
+            dma((7,)), dma((4,)), *two(3), *two(6), *two(8), *two(9),
             *two(3), *two(3), *two(2, 8), *two(2, 8), *two(2, 8), *two(2, 8), *two(2, 8), *two(8),
-            *two(3), *two(2, 8), *two(3),
+            *two(3), *two(2, 8), *two(5),
         ],
         compiler_params=pltpu.CompilerParams(
             collective_id=0, has_side_effects=True, vmem_limit_bytes=60 << 20
@@ -556,9 +624,9 @@
         moe_gain[None, :],
         cos,
         sin,
-        segment[:, None].astype(F32),
-        routes,
-        gates,
+        segment[None, :],
+        routes.T,
+        gates.T,
         page_table,
         w_latent.T,
         w_query,

time: 190 us -> 175 us (0.921)
  the two profiles are of different devices: /device:TPU:73 before, /device:TPU:1 now
where the time goes in v5:
time: 175 us; the launch traced here: 174 us
  Pallas kernels  169 us (97%)
  local copies, waits for them, and re-layouts  3.48 us (2%)
    pallas_call x1, Pallas kernels, local(): pl.pallas_call(layer_kernel, out_shape=(jax.ShapeDtypeStruct((TOK, D), BF...  169 us

profile of v5, /device:TPU:1, one launch (start us, length us, event | category | flops | bytes accessed | tf_op | source)
XLA Modules:
  0.0 174.3 jit_solution(10685832258644971833)
XLA Ops:
  0.7 0.1 pad.5.clone
  0.7 0.3 fusion
  1.1 0.8 maximum_maximum_fusion.1
  1.8 169.1 %shard_map.158 = (bf16[128,2048]{1,0:T(8,128)(2,1)}, bf16[32,576]{1,0:T(8,128)(2,1)}) custom-call(bf16[128,2048]{1,0:T(8,128)(2,1)} %hid_ref.1, f32[1,2048]{1,0:T(1,128)} %bitcast.12, f32[1,512]{1,0:T(1,128)} %bitcast.16, f32[1,2048]{1,0:T(1,128)} %bitcast.13, f32[128,128]{1,0:T(8,128)} %get-tuple-element.10.cos_ref, f32[128,128]{1,0:T(8,128)} %get-tuple-element.9.sin_ref, ...), custom_call_target="tpu_custom_call" | custom-call | tf_op jit(solution)/shard_map/pallas_call | solution.py:594
  170.9 1.5 reshape.18
  172.5 1.9 %copy.19 = bf16[128,2048]{1,0:T(8,128)(2,1)} copy(bf16[128,2048]{1,0:T(8,128)(2,1)} %get-tuple-element.13) | data formatting | bytes 1048576
  (3 shorter events, 0.0 us)

commit v6 on v5

--- a/solution.py
+++ b/solution.py
@@ -34,7 +34,7 @@
     return jnp.dot(a, b, preferred_element_type=F32)
 
 
-ORDER = ((0, 1), (7, 2), (6, 3), (5, 4))
+ORDER = ((7, 6), (4, 5), (3, 2), (1, 0))
 
 
 def nt(a, b):
@@ -103,15 +103,16 @@
     def push(self, c, ring, k):
         along_x = (c == 0) == (ring == 0)
         x, y, z = self.x, self.y, self.z
-        turn = 1 if k in (0, 2) else 3
+        turn = 1 if k in (0, 2, 4) else 3
         to = device(z, (x + turn) % 4, y, self.core) if along_x else device(z, x, (y + turn) % 4, self.core)
-        lo, n, step = ((0, NEAR, 0), (0, NEAR, 0), (*HALVES[0], 3), (*HALVES[1], 1))[k]
-        part = self.region(c, ring, lo, n, step)
-        return remote(part, part, self.ps.at[4 * ring + k], self.pr.at[4 * ring + k], to)
+        half, step = ((0, 0), (1, 0), (0, 3), (1, 1), (1, 0), (0, 0))[k]
+        part = self.region(c, ring, *HALVES[half], step)
+        return remote(part, part, self.ps.at[6 * ring + k], self.pr.at[6 * ring + k], to)
 
     def arrive(self, c, ring, k):
-        part = self.piece(c, 1 + 4 * ring + k)
-        remote(part, part, self.ps.at[4 * ring + k], self.pr.at[4 * ring + k], self.partner).wait_recv()
+        half, step = ((0, 3), (1, 1), (0, 2), (1, 2), (1, 3), (0, 1))[k]
+        part = self.region(c, ring, *HALVES[half], step)
+        remote(part, part, self.ps.at[6 * ring + k], self.pr.at[6 * ring + k], self.partner).wait_recv()
 
     def along_z(self, mine_ref):
         slot = lambda r: self.keys.at[r, self.x, self.y, self.core]
@@ -134,15 +135,15 @@
 
     def first_rings(self, c):
         self.share(c, 0).start()
-        self.push(c, 0, 0).start()
-        self.push(c, 0, 1).start()
-        for k in range(4):
+        for k in (0, 1, 4, 5):
+            self.push(c, 0, k).start()
+        for k in range(2):
             self.arrive(c, 0, k)
-            if k < 2:
-                self.push(c, 0, 2 + k).start()
-            if k == 3:
-                self.push(c, 1, 0).start()
-                self.push(c, 1, 1).start()
+            self.push(c, 0, 2 + k).start()
+        for k in (4, 5, 2, 3):
+            self.arrive(c, 0, k)
+        for k in (0, 1, 4, 5):
+            self.push(c, 1, k).start()
         for k in range(4):
             self.share(c, 1 + k).start()
         for i in range(5):
@@ -152,6 +153,8 @@
         for k in range(2):
             self.arrive(c, 1, k)
             self.push(c, 1, 2 + k).start()
+        for k in range(2):
+            self.arrive(c, 1, 4 + k)
             self.share(c, 5 + k).start()
         for i in (5, 6):
             self.shared(c, i)
@@ -169,7 +172,7 @@
         for i in range(9):
             self.share(c, i).wait_send()
         for ring in range(2):
-            for k in range(4):
+            for k in range(6):
                 self.push(c, ring, k).wait_send()
 
 
@@ -182,7 +185,7 @@
 def layer_kernel(
     hid_ref, again_ref, lgain_ref, mgain_ref, cos_ref, sin_ref, seg_ref, routes_ref, gates_ref, pages_ref,
     wl_hbm, wq_hbm, we_hbm, wo_hbm, wg_hbm, wu_hbm, wd_hbm, o_ref, cache_ref,
-    wl, wq, we, wo, wg, wu, wd, normed, lpart, lall, tagged, keys, ql, qm, qbuf, m_ref, l_ref, acc_ref, mixed,
+    wl, wq, we, wo, wg, wu, wd, normed, lpart, lall, tagged, keys, qf, qbuf, m_ref, l_ref, acc_ref, mixed,
     turn, pick, high, low, mix, apart, ain, res, outgoing, items, xin, pout, cin, ysend, yin, back, ret, acc, fin,
     w_sem, own_sem, ls, lr, zs_, zr_, ps, pr, cs, cr,
     rs, rr, a0s, a0r, as_, ar, fys, fyr, fps, fpr, fqs, fqr, xs, xr, ys, yr, b0s, b0r, bs, br, es, er,
@@ -275,7 +278,7 @@
     lane = lax.broadcasted_iota(jnp.int32, (tok, 128), 1)
     tagged[:, LATENT:] = jnp.where(lane == ROPE, seg_col, turned).astype(BF16)
 
-    scale = (NOPE + ROPE) ** (-0.5)
+    scale = (NOPE + ROPE) ** (-0.5) * 1.4426950408889634
 
     def work():
         page = jnp.zeros((PART, WIDTH), BF16)
@@ -295,9 +298,8 @@
                 h = 2 * k + i
                 rows = slice(h * tok, (h + 1) * tok)
                 key_w = we[:, h * (NOPE + VDIM) : h * (NOPE + VDIM) + NOPE]
-                ql[rows, :] = (nt(nope[i].astype(BF16), key_w) * scale).astype(BF16)
-                qm[rows, :] = (rotated(rope[i], cos_ref[...], sin_ref[...]) * scale).astype(BF16)
-        qm[HEADS * tok :, :] = (lax.broadcasted_iota(jnp.int32, (16, 128), 1) == ROPE).astype(F32).astype(BF16)
+                qf[rows, :LATENT] = (nt(nope[i].astype(BF16), key_w) * scale).astype(BF16)
+                qf[rows, LATENT:] = (rotated(rope[i], cos_ref[...], sin_ref[...]) * scale).astype(BF16)
         row = lax.broadcasted_iota(jnp.int32, (tok, 128), 0)
         below = (lane < row).astype(F32).astype(BF16)
         cell = lane // SLOTS
@@ -328,38 +330,42 @@
     next(first)
     work()
     rows = HEADS * tok
-    m_ref[...] = jnp.full_like(m_ref, -1e30)
-    l_ref[...] = jnp.zeros_like(l_ref)
-    acc_ref[...] = jnp.zeros_like(acc_ref)
-    qpos = seq * tok + lax.broadcasted_iota(jnp.int32, (rows, 1), 0) % tok
     qseg = jnp.concatenate([seg_col] * HEADS, axis=0)
+    at_seg = (lax.broadcasted_iota(jnp.int32, (16, 128), 1) == ROPE).astype(F32).astype(BF16)
+
+    def segments(block):
+        return nt(at_seg, block[:, LATENT:])[0:1]
+
+    block = tagged[...]
+    query = lax.broadcasted_iota(jnp.int32, (rows, 1), 0) % tok
+    ok = (qseg == segments(block)) & (lax.broadcasted_iota(jnp.int32, (1, tok), 1) <= query)
+    sc = jnp.where(ok, nt(qf[...], block), -1e30)
+    top = jnp.max(sc, axis=1, keepdims=True)
+    p = jnp.exp2(sc - top)
+    m_ref[...] = top
+    l_ref[...] = jnp.sum(p, axis=1, keepdims=True)
+    acc_ref[...] = dot(p.astype(BF16), block[:, :LATENT])
 
     def attend(color, line):
-        for lo, n in HALVES:
-            parts = []
-            for k in range(4):
-                xx = jnp.where(color == 0, k, line)
-                yy = jnp.where(color == 0, line, k)
-                parts.append(keys[pl.ds(lo, n), xx, yy, color].reshape(n * PART, WIDTH))
-            block = jnp.concatenate(parts, axis=0)
-            at = lax.broadcasted_iota(jnp.int32, (1, n * 128), 1)
-            turn_k = at // (n * PART)
-            plane = (z + 2 + lo + (at // PART) % n) % 8
-            kpos = plane * 1024 + color * PART + at % PART
-            kpos = kpos + jnp.where(color == 0, turn_k * 256 + line * 64, line * 256 + turn_k * 64)
-            c = block[:, :LATENT]
-            more = nt(qm[...], block[:, LATENT:])
-            sc = nt(ql[...], c) + more[:rows]
-            kseg = more[rows : rows + 1]
-            ok = (qseg == kseg) & (kpos <= qpos)
-            sc = jnp.where(ok, sc, -1e30)
-            m_old = m_ref[...]
-            m_new = jnp.maximum(m_old, jnp.max(sc, axis=1, keepdims=True))
-            p = jnp.where(ok, jnp.exp(sc - m_new), 0.0)
-            fade = jnp.exp(m_old - m_new)
-            l_ref[...] = l_ref[...] * fade + jnp.sum(p, axis=1, keepdims=True)
-            acc_ref[...] = acc_ref[...] * fade + dot(p.astype(BF16), c)
-            m_ref[...] = m_new
+        parts = []
+        for k in range(4):
+            xx = jnp.where(color == 0, k, line)
+            yy = jnp.where(color == 0, line, k)
+            parts.append(keys[:, xx, yy, color].reshape(NEAR * PART, WIDTH))
+        block = jnp.concatenate(parts, axis=0)
+        at = lax.broadcasted_iota(jnp.int32, (1, NEAR * 128), 1)
+        place = at // (NEAR * PART)
+        plane = (z + 2 + (at // PART) % NEAR) % 8
+        source = plane * 8 + jnp.where(color == 0, place * 2 + line // 2, line * 2 + place // 2)
+        kseg = jnp.where(source < seq, segments(block), -1.0)
+        sc = jnp.where(qseg == kseg, nt(qf[...], block), -1e30)
+        m_old = m_ref[...]
+        m_new = jnp.maximum(m_old, jnp.max(sc, axis=1, keepdims=True))
+        p = jnp.exp2(sc - m_new)
+        fade = jnp.exp2(m_old - m_new)
+        l_ref[...] = l_ref[...] * fade + jnp.sum(p, axis=1, keepdims=True)
+        acc_ref[...] = acc_ref[...] * fade + dot(p.astype(BF16), block[:, :LATENT])
+        m_ref[...] = m_new
 
     def attend_lines(steps):
         def one(t, carry):
@@ -602,7 +608,7 @@
         scratch_shapes=[
             space(144, D), space(D, 768), space(LATENT, 1024), space(512, D), space(ff, D), space(ff, D),
             space(ff, D), space(TOK, D), space(TOK, 256), space(3, TOK, 256), space(TOK, WIDTH),
-            space(NEAR, 4, 4, 2, PART, WIDTH), space(rows, LATENT), space(rows + 16, 128),
+            space(NEAR, 4, 4, 2, PART, WIDTH), space(rows, WIDTH),
             pltpu.VMEM((TOK, 768), F32), pltpu.VMEM((rows, 1), F32), pltpu.VMEM((rows, 1), F32),
             pltpu.VMEM((rows, LATENT), F32), space(rows, LATENT),
             pltpu.VMEM((TOK, 128), F32), space(*tables), space(*tables), space(*tables), space(*quarter),
@@ -610,7 +616,7 @@
             space(3, *quarter), space(*quarter), space(*chunks), space(4, *chunks), space(2 * TOK, D),
             space(4, *chunks), space(2, *chunks), space(*chunks), space(*chunks), space(*chunks), space(*chunks),
             pltpu.VMEM(quarter, F32), space(4, *quarter),
-            dma((7,)), dma((4,)), *two(3), *two(6), *two(8), *two(9),
+            dma((7,)), dma((4,)), *two(3), *two(6), *two(12), *two(9),
             *two(3), *two(3), *two(2, 8), *two(2, 8), *two(2, 8), *two(2, 8), *two(2, 8), *two(8),
             *two(3), *two(2, 8), *two(5),
         ],

time: 175 us -> 171 us (0.977)
  Pallas kernels: 169 us -> 165 us
    pallas_call x1, Pallas kernels: 169 us -> 165 us  [local(): pl.pallas_call(layer_kernel, out_shape=(jax.ShapeDtypeStruct((TOK, D), BF...]
where the time goes in v6:
time: 171 us; the launch traced here: 170 us
  Pallas kernels  165 us (96%)
  local copies, waits for them, and re-layouts  3.48 us (2%)
    pallas_call x1, Pallas kernels, local(): pl.pallas_call(layer_kernel, out_shape=(jax.ShapeDtypeStruct((TOK, D), BF...  165 us

profile of v6, /device:TPU:1, one launch (start us, length us, event | category | flops | bytes accessed | tf_op | source)
XLA Modules:
  0.0 170.3 jit_solution(10578272465508364875)
XLA Ops:
  0.7 0.1 pad.5.clone
  0.7 0.3 fusion
  1.1 0.8 maximum_maximum_fusion.1
  1.8 165.1 %shard_map.158 = (bf16[128,2048]{1,0:T(8,128)(2,1)}, bf16[32,576]{1,0:T(8,128)(2,1)}) custom-call(bf16[128,2048]{1,0:T(8,128)(2,1)} %hid_ref.1, f32[1,2048]{1,0:T(1,128)} %bitcast.12, f32[1,512]{1,0:T(1,128)} %bitcast.16, f32[1,2048]{1,0:T(1,128)} %bitcast.13, f32[128,128]{1,0:T(8,128)} %get-tuple-element.10.cos_ref, f32[128,128]{1,0:T(8,128)} %get-tuple-element.9.sin_ref, ...), custom_call_target="tpu_custom_call" | custom-call | tf_op jit(solution)/shard_map/pallas_call | solution.py:600
  166.9 1.5 reshape.18
  168.5 1.9 %copy.19 = bf16[128,2048]{1,0:T(8,128)(2,1)} copy(bf16[128,2048]{1,0:T(8,128)(2,1)} %get-tuple-element.13) | data formatting | bytes 1048576
  (3 shorter events, 0.0 us)

commit v7 on v6

--- a/solution.py
+++ b/solution.py
@@ -34,7 +34,7 @@
     return jnp.dot(a, b, preferred_element_type=F32)
 
 
-ORDER = ((7, 6), (4, 5), (3, 2), (1, 0))
+ORDER = ((7, 1), (4, 0), (5, 3), (6, 2))
 
 
 def nt(a, b):
@@ -186,7 +186,7 @@
     hid_ref, again_ref, lgain_ref, mgain_ref, cos_ref, sin_ref, seg_ref, routes_ref, gates_ref, pages_ref,
     wl_hbm, wq_hbm, we_hbm, wo_hbm, wg_hbm, wu_hbm, wd_hbm, o_ref, cache_ref,
     wl, wq, we, wo, wg, wu, wd, normed, lpart, lall, tagged, keys, qf, qbuf, m_ref, l_ref, acc_ref, mixed,
-    turn, pick, high, low, mix, apart, ain, res, outgoing, items, xin, pout, cin, ysend, yin, back, ret, acc, fin,
+    turn, pick, high, low, mix, apart, asend, ain, res, outgoing, items, xin, pout, cin, ysend, yin, back, ret, acc, fin,
     w_sem, own_sem, ls, lr, zs_, zr_, ps, pr, cs, cr,
     rs, rr, a0s, a0r, as_, ar, fys, fyr, fps, fpr, fqs, fqr, xs, xr, ys, yr, b0s, b0r, bs, br, es, er,
 ):
@@ -402,13 +402,15 @@
     loads[3].wait()
     for q in range(4):
         apart[q] = dot(mix[...], wo[:, q * 512 : (q + 1) * 512]).astype(BF16)
-    for d in range(1, 4):
-        q = (head + d) % 4
-        push(apart.at[q], ain.at[d - 1], rs.at[d - 1], rr.at[d - 1], (seq, q))
-    total = apart[head].astype(F32)
-    for d in range(1, 4):
-        arrive(ain.at[d - 1], rr.at[d - 1])
-        total = total + ain[d - 1].astype(F32)
+    for side in range(2):
+        push(apart.at[side * 2 + 1 - core], ain.at[side], rs.at[side], rr.at[side], partner)
+    for side in range(2):
+        arrive(ain.at[side], rr.at[side])
+    asend[...] = (apart[q_across].astype(F32) + ain[1 - yl].astype(F32)).astype(BF16)
+    push(asend, ain.at[2], rs.at[2], rr.at[2], across)
+    total = apart[head].astype(F32) + ain[yl].astype(F32)
+    arrive(ain.at[2], rr.at[2])
+    total = total + ain[2].astype(F32)
     own = hid_ref[:, pl.ds(pl.multiple_of(head * 512, 512), 512)].astype(F32)
     res[...] = (own + total).astype(BF16)
 
@@ -612,7 +614,7 @@
             pltpu.VMEM((TOK, 768), F32), pltpu.VMEM((rows, 1), F32), pltpu.VMEM((rows, 1), F32),
             pltpu.VMEM((rows, LATENT), F32), space(rows, LATENT),
             pltpu.VMEM((TOK, 128), F32), space(*tables), space(*tables), space(*tables), space(*quarter),
-            space(4, *quarter),
+            space(4, *quarter), space(*quarter),
             space(3, *quarter), space(*quarter), space(*chunks), space(4, *chunks), space(2 * TOK, D),
             space(4, *chunks), space(2, *chunks), space(*chunks), space(*chunks), space(*chunks), space(*chunks),
             pltpu.VMEM(quarter, F32), space(4, *quarter),

time: 171 us -> 161 us (0.942)
  Pallas kernels: 165 us -> 155 us
    pallas_call x1, Pallas kernels: 165 us -> 155 us  [local(): pl.pallas_call(layer_kernel, out_shape=(jax.ShapeDtypeStruct((TOK, D), BF...]
where the time goes in v7:
time: 161 us; the launch traced here: 160 us
  Pallas kernels  155 us (96%)
  local copies, waits for them, and re-layouts  3.48 us (2%)
    pallas_call x1, Pallas kernels, local(): pl.pallas_call(layer_kernel, out_shape=(jax.ShapeDtypeStruct((TOK, D), BF...  155 us

profile of v7, /device:TPU:1, one launch (start us, length us, event | category | flops | bytes accessed | tf_op | source)
XLA Modules:
  0.0 160.4 jit_solution(7344109729838021465)
XLA Ops:
  0.7 0.1 pad.5.clone
  0.7 0.3 fusion
  1.1 0.8 maximum_maximum_fusion.1
  1.8 155.2 %shard_map.158 = (bf16[128,2048]{1,0:T(8,128)(2,1)}, bf16[32,576]{1,0:T(8,128)(2,1)}) custom-call(bf16[128,2048]{1,0:T(8,128)(2,1)} %hid_ref.1, f32[1,2048]{1,0:T(1,128)} %bitcast.12, f32[1,512]{1,0:T(1,128)} %bitcast.16, f32[1,2048]{1,0:T(1,128)} %bitcast.13, f32[128,128]{1,0:T(8,128)} %get-tuple-element.10.cos_ref, f32[128,128]{1,0:T(8,128)} %get-tuple-element.9.sin_ref, ...), custom_call_target="tpu_custom_call" | custom-call | tf_op jit(solution)/shard_map/pallas_call | solution.py:602
  157.0 1.5 reshape.18
  158.5 1.9 %copy.19 = bf16[128,2048]{1,0:T(8,128)(2,1)} copy(bf16[128,2048]{1,0:T(8,128)(2,1)} %get-tuple-element.13) | data formatting | bytes 1048576
  (3 shorter events, 0.0 us)

commit v8 on v7

--- a/solution.py
+++ b/solution.py
@@ -531,8 +531,8 @@
 
     a, b, c, d, e = stage_a, stage_b, stage_c, stage_d, stage_e
     for stage, g in (
-        (a, 0), (b, 0), (a, 1), (c, 0), (b, 1), (d, 0), (a, 2), (c, 1), (e, 0), (b, 2),
-        (d, 1), (a, 3), (c, 2), (e, 1), (b, 3), (d, 2), (c, 3), (e, 2), (d, 3), (e, 3),
+        (a, 0), (b, 0), (c, 0), (a, 1), (d, 0), (b, 1), (c, 1), (e, 0), (a, 2), (d, 1),
+        (b, 2), (c, 2), (e, 1), (a, 3), (d, 2), (b, 3), (c, 3), (e, 2), (d, 3), (e, 3),
     ):
         stage(g)
 

time: 161 us -> 169 us (1.050)
  Pallas kernels: 155 us -> 162 us
    pallas_call x1, Pallas kernels: 155 us -> 162 us  [local(): pl.pallas_call(layer_kernel, out_shape=(jax.ShapeDtypeStruct((TOK, D), BF...]
where the time goes in v8:
time: 169 us; the launch traced here: 167 us
  Pallas kernels  162 us (96%)
  local copies, waits for them, and re-layouts  3.48 us (2%)
    pallas_call x1, Pallas kernels, local(): pl.pallas_call(layer_kernel, out_shape=(jax.ShapeDtypeStruct((TOK, D), BF...  162 us

profile of v8, /device:TPU:1, one launch (start us, length us, event | category | flops | bytes accessed | tf_op | source)
XLA Modules:
  0.0 167.4 jit_solution(12443785021758010504)
XLA Ops:
  0.7 0.1 pad.5.clone
  0.7 0.3 fusion
  1.1 0.8 maximum_maximum_fusion.1
  1.8 162.2 %shard_map.158 = (bf16[128,2048]{1,0:T(8,128)(2,1)}, bf16[32,576]{1,0:T(8,128)(2,1)}) custom-call(bf16[128,2048]{1,0:T(8,128)(2,1)} %hid_ref.1, f32[1,2048]{1,0:T(1,128)} %bitcast.12, f32[1,512]{1,0:T(1,128)} %bitcast.16, f32[1,2048]{1,0:T(1,128)} %bitcast.13, f32[128,128]{1,0:T(8,128)} %get-tuple-element.10.cos_ref, f32[128,128]{1,0:T(8,128)} %get-tuple-element.9.sin_ref, ...), custom_call_target="tpu_custom_call" | custom-call | tf_op jit(solution)/shard_map/pallas_call | solution.py:602
  164.0 1.5 reshape.18
  165.5 1.9 %copy.19 = bf16[128,2048]{1,0:T(8,128)(2,1)} copy(bf16[128,2048]{1,0:T(8,128)(2,1)} %get-tuple-element.13) | data formatting | bytes 1048576
  (3 shorter events, 0.0 us)
